TPU v7x, 128 devices: a whole 4x4x4 slice. The times are simulated.
128 devices in a mesh: dp: 8 (over z, core), expert: 16 (over x, y).
Axes of the slice: x: 4, y: 4, z: 4, core: 2. Of those that a mesh axis runs over, the one named last changes fastest.
Arguments:
- tokens: bfloat16 [8192, 4096], P(('dp', 'expert')), may hold values from -6 to 6
- queries: bfloat16 [8192, 4096], P(('dp', 'expert')), may hold values from -64 to 64
- keys_values: bfloat16 [8192, 2048], P(('dp', 'expert')), may hold values from -4 to 4
- scan_input: bfloat16 [8192, 4096], P(('dp', 'expert')), may hold values from -6 to 6
- state_maps: float32 [8192, 32], P(('dp', 'expert')), may hold values from -1.5 to 1.5
- step_size: float32 [8192, 64], P(('dp', 'expert')), may hold values from 0.05 to 0.5
- step_decay: float32 [8192, 64], P(('dp', 'expert')), may hold values from -1.2 to 0
- block_pool: bfloat16 [1024, 16, 2048], P(('dp', 'expert')), may hold values from -5 to 5
- state_pool: float32 [256, 65536], P(('dp', 'expert')), may hold values from -5 to 5
- block_holder: int32 [128, 16], P(('dp', 'expert')), may hold values from 0 to 7, as said below
- block_index: int32 [128, 16], P(('dp', 'expert')), may hold values from 0 to 7
- cached_blocks: int32 [128], P(('dp', 'expert')), may hold values from 1 to 16, as said below
- state_holder: int32 [128], P(('dp', 'expert')), may hold values from 0 to 7
- state_index: int32 [128], P(('dp', 'expert')), may hold values from 0 to 1
- norm_gain: float32 [4096], replicated, may hold values from 0.1 to 1.9
- router_weight: bfloat16 [4096, 16], replicated, may hold values from -0.09375 to 0.09375
- expert_ids: int32 [8192, 2], P(('dp', 'expert')), may hold values from 0 to 15, all different within a row; in each aligned block of 64 rows (0 to 63, 64 to 127, ...) at most 8 rows name the same one
- up_weight: bfloat16 [16, 4096, 7168], P('expert', None, 'dp'), may hold values from -0.09375 to 0.09375
- down_weight: bfloat16 [16, 7168, 4096], P('expert', 'dp'), may hold values from -0.0625 to 0.0625
Outputs:
- layer_out: bfloat16 [8192, 4096], P(('dp', 'expert'))
- final_state: float32 [128, 65536], P(('dp', 'expert'))
Inputs may be any that keep to these rules, and one draw needn't show every extreme that they name: `block_holder`: each row names every holder exactly 2 times over its 16 entries, so at most 2 of a request's cached blocks sit on one holder. `cached_blocks`: some request caches 16 blocks. `expert_ids`: the two experts of a token differ, and each expert is named by exactly 8 rows of one device.
All inputs are finite; a program needn't handle non-finite values.
Results may differ from a plain program's by a relative error of at most 0.0095.
Values may be sent and summed in bfloat16 or wider, within the bound.
A program may use at most 128 MiB of HBM per device.

v0:
```python
import jax
import jax.numpy as jnp
from jax import lax
from jax.sharding import PartitionSpec as P

HEADS = 32
KV_HEADS = 8
HEAD = 128
SSM_HEADS = 64
SSM_DIM = 64
NSTATE = 16
BLOCK = 16


def attend(queries, keys_values, prefix, cached_count):
    length = queries.shape[0]
    groups = HEADS // KV_HEADS
    past_len = prefix.shape[0] * prefix.shape[1]
    joined = jnp.concatenate([prefix.reshape(past_len, -1), keys_values], 0)
    joined = joined.reshape(past_len + length, 2, KV_HEADS, HEAD)
    key_rows = joined[:, 0]
    values = joined[:, 1]
    grouped = queries.reshape(length, KV_HEADS, groups, HEAD)
    scores = jnp.einsum(
        "tgqd,kgd->gqtk", grouped, key_rows, preferred_element_type=jnp.float32
    ) * HEAD ** (-0.5)
    places = jnp.arange(past_len + length, dtype=jnp.int32)
    tokens_at = jnp.arange(length, dtype=jnp.int32)
    visible = jnp.where(
        places[None, :] < past_len,
        places[None, :] < cached_count * BLOCK,
        places[None, :] - past_len <= tokens_at[:, None],
    )
    scores = jnp.where(visible, scores, -jnp.inf)
    row_max = jnp.max(scores, axis=-1, keepdims=True)
    weights = jnp.exp(scores - row_max)
    weights = (weights / jnp.sum(weights, axis=-1, keepdims=True)).astype(jnp.bfloat16)
    output = jnp.einsum("gqtk,kgd->tgqd", weights, values, preferred_element_type=jnp.float32)
    return output.reshape(length, -1)


def state_block(inputs, state_maps, steps, decays, start_flat):
    length = inputs.shape[0]
    values = inputs.astype(jnp.float32).reshape(length, SSM_HEADS, SSM_DIM)
    entry_maps = state_maps[:, :NSTATE]
    readout = state_maps[:, NSTATE:]
    running = jnp.cumsum(decays, axis=0)
    places = jnp.arange(length, dtype=jnp.int32)
    causal = (places[:, None] >= places[None, :])[:, :, None]
    spread = running[:, None, :] - running[None, :, :]
    fading = jnp.where(causal, jnp.exp(jnp.where(causal, spread, 0.0)), 0.0)
    intersection = jnp.dot(readout, entry_maps.T)
    mixing = fading * intersection[:, :, None] * steps[None, :, :]
    output = jnp.einsum("tsh,shp->thp", mixing, values)
    start_state = start_flat.reshape(SSM_HEADS, SSM_DIM, NSTATE)
    output = output + jnp.exp(running)[:, :, None] * jnp.einsum("tn,hpn->thp", readout, start_state)
    last_sum = running[-1]
    weight = jnp.exp(last_sum[None, :] - running) * steps
    final_state = jnp.exp(last_sum)[:, None, None] * start_state + jnp.einsum(
        "sh,shp,sn->hpn", weight, values, entry_maps
    )
    return (output.reshape(length, -1), final_state.reshape(-1))


def apply_expert(row_block, up_local, down_local):
    flattened = row_block.reshape(-1, row_block.shape[-1])
    hidden = jax.nn.silu(jnp.dot(flattened, up_local, preferred_element_type=jnp.float32)).astype(
        jnp.bfloat16
    )
    partial_value = jnp.dot(hidden, down_local, preferred_element_type=jnp.float32)
    return partial_value.reshape(row_block.shape)


def local(
    tokens,
    queries,
    keys_values,
    scan_input,
    state_maps,
    step_size,
    step_decay,
    block_pool,
    state_pool,
    block_holder,
    block_index,
    cached_blocks,
    state_holder,
    state_index,
    norm_gain,
    router_weight,
    expert_ids,
    up_weight,
    down_weight,
):
    dp_size = lax.axis_size("dp")
    holders = block_holder[0]
    indices = block_index[0]
    cached_count = cached_blocks[0]
    entries = holders.shape[0]
    places = jnp.arange(entries, dtype=jnp.int32)
    usable = places < cached_count
    peer_ids = jnp.arange(dp_size, dtype=jnp.int32)
    state_owner = state_holder[0]
    state_wanted = jnp.where(peer_ids == state_owner, state_index[0], 0)[:, None]
    pooled = lax.all_gather(block_pool, "dp", axis=0, tiled=True)
    row_ids = jnp.where(usable, holders * block_pool.shape[0] + indices, 0)
    prefix = pooled[row_ids]
    state_asked = lax.all_to_all(state_wanted, "dp", split_axis=0, concat_axis=0, tiled=True)
    sent_states = state_pool[state_asked.reshape(-1)][:, None, :]
    arrived_states = lax.all_to_all(
        sent_states.astype(jnp.bfloat16), "dp", split_axis=0, concat_axis=0, tiled=True
    ).astype(sent_states.dtype)
    start_flat = arrived_states[state_owner, 0]
    attended = attend(queries, keys_values, prefix, cached_count)
    ssm_out, final_state = state_block(scan_input, state_maps, step_size, step_decay, start_flat)
    mixed_rows = (tokens.astype(jnp.float32) + (attended + ssm_out)).astype(jnp.bfloat16)
    mixed_wide = lax.optimization_barrier(mixed_rows).astype(jnp.float32)
    normed = (
        mixed_wide
        * lax.rsqrt(jnp.mean(mixed_wide * mixed_wide, axis=-1, keepdims=True) + 1e-05)
        * norm_gain
    ).astype(jnp.bfloat16)
    logits = jnp.dot(normed, router_weight, preferred_element_type=jnp.float32)
    chosen = jnp.take_along_axis(logits, expert_ids, axis=1)
    lifted = jax.nn.sigmoid(chosen)
    gate_values = lifted / jnp.sum(lifted, axis=1, keepdims=True)
    experts = router_weight.shape[1]
    expert_list = expert_ids.reshape(-1)
    capacity = expert_list.shape[0] // experts
    onehot = (expert_list[:, None] == jnp.arange(experts, dtype=jnp.int32)[None, :]).astype(
        jnp.int32
    )
    before = jnp.cumsum(onehot, axis=0) - onehot
    expert_slot = jnp.sum(before * onehot, axis=1)
    target = expert_list * capacity + expert_slot
    owner_ids = jnp.arange(expert_list.shape[0], dtype=jnp.int32) // 2
    source = jnp.sum(
        jnp.where(
            target[:, None] == jnp.arange(experts * capacity, dtype=jnp.int32)[None, :],
            owner_ids[:, None],
            0,
        ),
        axis=0,
    )
    dispatch = normed[source].reshape(experts, capacity, -1)
    up_local = up_weight[0]
    down_local = down_weight[0]
    received = lax.all_to_all(dispatch, "expert", split_axis=0, concat_axis=0, tiled=True)
    gathered = lax.all_gather(received, "dp", axis=0, tiled=True)
    own_sums = lax.psum_scatter(
        apply_expert(gathered, up_local, down_local).astype(jnp.bfloat16),
        "dp",
        scatter_dimension=0,
        tiled=True,
    ).astype(jnp.float32)
    summed = lax.all_to_all(
        own_sums.astype(jnp.bfloat16), "expert", split_axis=0, concat_axis=0, tiled=True
    ).astype(own_sums.dtype)
    picked = summed.reshape(experts * capacity, -1)[target]
    combined = jnp.sum(picked.reshape(tokens.shape[0], 2, -1) * gate_values[:, :, None], axis=1)
    layer_out = (mixed_wide + combined).astype(jnp.bfloat16)
    return (layer_out, final_state[None, :])


def solution(mesh):
    placed = (
        P(("dp", "expert"), None),
        P(("dp", "expert"), None),
        P(("dp", "expert"), None),
        P(("dp", "expert"), None),
        P(("dp", "expert"), None),
        P(("dp", "expert"), None),
        P(("dp", "expert"), None),
        P(("dp", "expert"), None, None),
        P(("dp", "expert"), None),
        P(("dp", "expert"), None),
        P(("dp", "expert"), None),
        P(("dp", "expert")),
        P(("dp", "expert")),
        P(("dp", "expert")),
        P(),
        P(),
        P(("dp", "expert"), None),
        P("expert", None, "dp"),
        P("expert", "dp", None),
    )
    return jax.shard_map(
        local,
        mesh=mesh,
        in_specs=placed,
        out_specs=(P(("dp", "expert"), None), P(("dp", "expert"), None)),
        check_vma=False,
    )
```

profile of v0, /device:TPU:0, one launch (start us, length us, event | category | flops | bytes accessed | tf_op | source)
XLA Modules:
  0.0 272.0 jit_solution(3783072387723759270)
XLA Ops:
  7.2 0.7 all-gather.3.cloned.1.call-update
  9.2 0.6 compare_select_fusion
  9.8 5.4 %all-to-all-start = ((s32[8,1,1]{2,1,0:T(1,128)}), s32[8,1,1]{2,1,0:T(1,128)S(1)}, u32[]{:S(2)}, u32[]{:S(2)}) async-start(s32[8,1,1]{2,1,0:T(1,128)} %compare_select_fusion), calls=%async_computation | async-start | bytes 8192 | tf_op jit(solution)/shard_map/all_to_all | solution.py:108
  15.9 0.8 copy.164
  16.8 0.9 reduce_window_sum.22
  17.9 0.6 iota_add_fusion
  18.5 0.7 fusion.58
  19.1 0.6 pad_clamp_fusion.3
  20.1 0.8 exponential_multiply_fusion
  20.9 0.2 reduce
  21.1 0.6 pad_clamp_fusion.1
  21.7 1.3 gather_fusion.1
  23.0 0.5 broadcast.287
  23.5 1.4 reduce.7
  25.0 1.9 reshape.336
  26.9 4.9 %all-to-all-start.1 = ((bf16[8,2,32768]{2,1,0:T(2,128)(2,1)}), bf16[8,2,32768]{2,1,0:T(2,128)(2,1)S(1)}, u32[]{:S(2)}, u32[]{:S(2)}) async-start(bf16[8,2,32768]{2,1,0:T(2,128)(2,1)} %reshape.336), calls=%async_computation.1 | async-start | bytes 2097152 | tf_op jit(solution)/shard_map/all_to_all | solution.py:110
  31.8 0.2 all-gather.5.cloned.1.call-start
  32.0 0.6 iota_compare_fusion.4
  32.7 0.7 copy.157
  33.5 0.4 reshape.267
  33.9 1.1 reshape.269
  35.1 0.7 fusion.48
  36.0 4.3 %fusion.11 = f32[64,64,64]{2,1,0:T(8,128)} fusion(f32[64,64]{0,1:T(8,128)} %copy.157, f32[64,64]{1,0:T(8,128)S(1)} %fusion.52, f32[64,64]{0,1:T(8,128)S(1)} %copy.155, pred[64,64]{1,0:T(8,128)(4,1)S(1)} %iota_compare_fusion.3, bf16[64,64,64]{2,1,0:T(8,128)(2,1)S(1)} %reshape.269), kind=kOutput, calls=%fused_computation.19 | convolution fusion | flops 34865152 | bytes 1626112 | tf_op jit(solution)/shard_map/tsh,shp->thp/dot_general | solution.py:54
  40.3 14.1 %all-to-all-done.1 = bf16[8,2,32768]{2,1,0:T(2,128)(2,1)S(1)} async-done(((bf16[8,2,32768]{2,1,0:T(2,128)(2,1)}), bf16[8,2,32768]{2,1,0:T(2,128)(2,1)S(1)}, u32[]{:S(2)}, u32[]{:S(2)}) %all-to-all-start.1) | async-done | bytes 1048608 | tf_op jit(solution)/shard_map/all_to_all | solution.py:110
  54.3 3.5 %reshape.337 = bf16[8,1,65536]{2,1,0:T(2,128)(2,1)} reshape(bf16[8,2,32768]{2,1,0:T(2,128)(2,1)S(1)} %all-to-all-done.1) | data formatting | bytes 2097152
  57.8 1.7 dynamic-slice_reduce_fusion
  59.5 0.7 reshape_squeeze.5
  60.2 2.5 fusion.10
  62.7 1.2 copy.163
  64.0 1.6 reshape.270
  65.6 2.9 %gather_fusion = bf16[16,16,2048]{2,1,0:T(8,128)(2,1)S(1)} fusion(bf16[64,16,2048]{2,1,0:T(8,128)(2,1)} %all-gather.3.cloned.1.call-done, s32[1024]{0:T(1024)} %pad_clamp_fusion.3), kind=kCustom, calls=%fused_computation | custom fusion | bytes 2097216 | tf_op jit(solution)/shard_map/gather | solution.py:107
  68.5 0.2 copy.179
  68.8 0.3 copy_dynamic-update-slice_fusion
  69.1 0.6 fusion.42
  69.7 1.4 fusion.64
  71.1 0.9 fusion.28
  72.0 1.7 copy.154
  73.7 1.6 reshape.268
  75.5 0.2 fusion.30
  75.7 0.4 copy-done.11
  76.1 0.2 fusion.32
  76.3 1.3 gather_fusion.2
  77.6 23.7 %all_to_all.24 = bf16[16,8,4096]{2,1,0:T(8,128)(2,1)} all-to-all(bf16[16,8,4096]{2,1,0:T(8,128)(2,1)S(1)} %bitcast.117), channel_id=1, replica_groups=mesh['dp'=8,'expert'=16] {'expert'}, dimensions={0} | all-to-all | bytes 2097152 | tf_op jit(solution)/shard_map/all_to_all | solution.py:148
  101.3 46.6 %all-gather.5.cloned.1.call-done = bf16[128,8,4096]{2,1,0:T(8,128)(2,1)} async-done(((bf16[16,8,4096]{2,1,0:T(8,128)(2,1)}), bf16[128,8,4096]{2,1,0:T(8,128)(2,1)}) %all-gather.5.cloned.1.call-update) | async-done | bytes 8388624 | tf_op jit(solution)/shard_map/all_gather | solution.py:149
  147.9 13.7 %fusion.23 = bf16[128,8,896]{2,1,0:T(8,128)(2,1)S(1)} fusion(bf16[1,4096,896]{2,1,0:T(8,128)(2,1)} %param.36, bf16[128,8,4096]{2,1,0:T(8,128)(2,1)} %all-gather.5.cloned.1.call-done), kind=kOutput, calls=%fused_computation.34 | convolution fusion | flops 7520780288 | bytes 17563648 | tf_op jit(solution)/shard_map/dot_general | solution.py:67
  161.6 14.1 %convolution_convert_fusion = bf16[128,8,4096]{2,0,1:T(8,128)(2,1)} fusion(bf16[1,896,4096]{2,1,0:T(8,128)(2,1)} %param.37, bf16[128,8,896]{2,1,0:T(8,128)(2,1)S(1)} %fusion.23), kind=kOutput, calls=%fused_computation.8 | convolution fusion | flops 7520387072 | bytes 17563648 | tf_op jit(solution)/shard_map/dot_general | solution.py:70
  175.7 0.7 copy-done.12
  177.0 51.6 %reduce-scatter.2.cloned.1.call-done = bf16[16,8,4096]{2,0,1:T(8,128)(2,1)} async-done(((bf16[128,8,4096]{2,0,1:T(8,128)(2,1)}), bf16[16,8,4096]{2,0,1:T(8,128)(2,1)}) %reduce-scatter.2.cloned.1.call-update) | async-done | bytes 1048592 | tf_op jit(solution)/shard_map/reduce_scatter | solution.py:150
  228.6 2.8 %copy.166 = bf16[16,8,4096]{2,1,0:T(8,128)(2,1)} copy(bf16[16,8,4096]{2,0,1:T(8,128)(2,1)} %reduce-scatter.2.cloned.1.call-done) | data formatting | bytes 2097152 | tf_op jit(solution)/shard_map/reduce_scatter | solution.py:150
  231.4 6.9 %all-to-all-start.3 = ((bf16[16,8,4096]{2,1,0:T(8,128)(2,1)}), bf16[16,8,4096]{2,1,0:T(8,128)(2,1)}, u32[]{:S(2)}, u32[]{:S(2)}) async-start(bf16[16,8,4096]{2,1,0:T(8,128)(2,1)} %copy.166), calls=%async_computation.4 | async-start | bytes 2097152 | tf_op jit(solution)/shard_map/all_to_all | solution.py:156
  238.2 1.7 convert_reduce_fusion
  240.0 0.6 reshape_squeeze.6
  240.6 1.4 copy.171
  242.0 3.0 %fusion.29 = f32[64,64,16]{1,2,0:T(8,128)} fusion(bf16[64,64,64]{2,1,0:T(8,128)(2,1)} %copy-done.3, f32[64,64,16]{1,2,0:T(8,128)} %copy.171, f32[64,16]{0,1:T(8,128)S(1)} %slice-done, f32[64,64]{0,1:T(8,128)S(1)} %copy.172, f32[64]{0:T(128)S(1)} %fusion.62), kind=kOutput, calls=%fused_computation.37 | convolution fusion | flops 8585216 | bytes 1069312 | tf_op jit(solution)/shard_map/sh,shp,sn->hpn/dot_general | solution.py:59
  245.0 1.7 copy.174
  246.7 1.5 broadcast_in_dim_reshape.4
  248.1 0.2 fusion.65
  248.4 1.3 gather_fusion.4
  250.1 4.8 %all-to-all-done.3 = bf16[16,8,4096]{2,1,0:T(8,128)(2,1)} async-done(((bf16[16,8,4096]{2,1,0:T(8,128)(2,1)}), bf16[16,8,4096]{2,1,0:T(8,128)(2,1)}, u32[]{:S(2)}, u32[]{:S(2)}) %all-to-all-start.3) | async-done | bytes 1048608 | tf_op jit(solution)/shard_map/all_to_all | solution.py:156
  254.9 1.4 bitcast_convert_fusion
  256.3 2.6 gather_fusion.3
  258.9 2.5 reshape.276
  261.4 3.1 %multiply_reduce_fusion = f32[64,4096]{1,0:T(8,128)S(1)} fusion(f32[64,2,4096]{2,1,0:T(2,128)S(1)} %reshape.276, f32[64,2]{1,0:T(8,128)S(1)} %copy.170), kind=kLoop, calls=%fused_computation.18 | loop fusion | flops 786432 | bytes 3146240 | tf_op jit(solution)/shard_map/reduce_sum | solution.py:160
  264.6 0.9 fusion.33
  (69 shorter events, 2.4 us)
Async XLA Ops:
  7.2 14.6 %copy-start = (f32[2,65536]{1,0:T(2,128)S(1)}, f32[2,65536]{1,0:T(2,128)}, u32[]{:S(2)}) copy-start(f32[2,65536]{1,0:T(2,128)} %param.27) | copy-start | bytes 1572868
  7.2 58.4 %all-gather.3.cloned.1.call-start = ((), (), s32[]{:S(2)}) async-start(), calls=%async_computation.5 | async-start | bytes 4718592 | tf_op jit(solution)/shard_map/all_gather | solution.py:105
  9.8 11.1 %all-to-all-start = ((s32[8,1,1]{2,1,0:T(1,128)}), s32[8,1,1]{2,1,0:T(1,128)S(1)}, u32[]{:S(2)}, u32[]{:S(2)}) async-start(s32[8,1,1]{2,1,0:T(1,128)} %compare_select_fusion), calls=%async_computation | async-start | bytes 8192 | tf_op jit(solution)/shard_map/all_to_all | solution.py:108
  19.9 1.8 copy-start.13
  24.9 7.8 %copy-start.8 = (f32[64,64]{1,0:T(8,128)S(1)}, f32[64,64]{1,0:T(8,128)}, u32[]{:S(2)}) copy-start(f32[64,64]{1,0:T(8,128)} %param.24) | copy-start | bytes 49156
  25.0 8.5 %copy-start.7 = (bf16[64,2048]{1,0:T(8,128)(2,1)S(1)}, bf16[64,2048]{1,0:T(8,128)(2,1)}, u32[]{:S(2)}) copy-start(bf16[64,2048]{1,0:T(8,128)(2,1)} %param.21) | copy-start | bytes 786436
  26.9 6.7 %copy-start.5 = (bf16[64,4096]{1,0:T(8,128)(2,1)S(1)}, bf16[64,4096]{1,0:T(8,128)(2,1)}, u32[]{:S(2)}) copy-start(bf16[64,4096]{1,0:T(8,128)(2,1)} %param.20) | copy-start | bytes 1572868
  26.9 7.1 %copy-start.4 = (bf16[64,4096]{1,0:T(8,128)(2,1)S(1)}, bf16[64,4096]{1,0:T(8,128)(2,1)}, u32[]{:S(2)}) copy-start(bf16[64,4096]{1,0:T(8,128)(2,1)} %param.22) | copy-start | bytes 1572868
  26.9 27.5 %all-to-all-start.1 = ((bf16[8,2,32768]{2,1,0:T(2,128)(2,1)}), bf16[8,2,32768]{2,1,0:T(2,128)(2,1)S(1)}, u32[]{:S(2)}, u32[]{:S(2)}) async-start(bf16[8,2,32768]{2,1,0:T(2,128)(2,1)} %reshape.336), calls=%async_computation.1 | async-start | bytes 2097152 | tf_op jit(solution)/shard_map/all_to_all | solution.py:110
  31.8 4.0 %copy-start.10 = (f32[64,32]{0,1:T(8,128)S(1)}, f32[64,32]{0,1:T(8,128)}, u32[]{:S(2)}) copy-start(f32[64,32]{0,1:T(8,128)} %param.23) | copy-start | bytes 24580
  31.8 116.1 %all-gather.5.cloned.1.call-start = ((), (), s32[]{:S(2)}) async-start(), calls=%async_computation.6 | async-start | bytes 9437184 | tf_op jit(solution)/shard_map/all_gather | solution.py:149
  35.1 5.2 %copy-start.3 = (bf16[64,64,64]{2,1,0:T(8,128)(2,1)}, bf16[64,64,64]{2,1,0:T(8,128)(2,1)S(1)}, u32[]{:S(2)}) copy-start(bf16[64,64,64]{2,1,0:T(8,128)(2,1)S(1)} %reshape.269) | copy-start | bytes 1572868
  72.0 3.4 %copy-start.2 = (f32[64,4096]{1,0:T(8,128)S(1)}, f32[64,4096]{1,0:T(8,128)}, u32[]{:S(2)}) copy-start(f32[64,4096]{1,0:T(8,128)} %reshape.270) | copy-start | bytes 3145732
  72.0 3.4 %copy-start.6 = (bf16[64,4096]{1,0:T(8,128)(2,1)S(1)}, bf16[64,4096]{1,0:T(8,128)(2,1)}, u32[]{:S(2)}) copy-start(bf16[64,4096]{1,0:T(8,128)(2,1)} %param.19) | copy-start | bytes 1572868
  75.4 0.7 copy-start.11
  101.3 127.3 %reduce-scatter.2.cloned.1.call-start = ((), (), s32[]{:S(2)}) async-start(), calls=%async_computation.7 | async-start | bytes 9437184 | tf_op jit(solution)/shard_map/reduce_scatter | solution.py:150
  175.7 0.7 copy-start.12
  175.7 1.3 copy-start.14
  231.4 23.5 %all-to-all-start.3 = ((bf16[16,8,4096]{2,1,0:T(8,128)(2,1)}), bf16[16,8,4096]{2,1,0:T(8,128)(2,1)}, u32[]{:S(2)}, u32[]{:S(2)}) async-start(bf16[16,8,4096]{2,1,0:T(8,128)(2,1)} %copy.166), calls=%async_computation.4 | async-start | bytes 2097152 | tf_op jit(solution)/shard_map/all_to_all | solution.py:156
  240.0 2.0 slice-start
  245.0 3.2 %copy-start.9 = (bf16[4096,16]{0,1:T(8,128)(2,1)S(1)}, bf16[4096,16]{0,1:T(8,128)(2,1)}, u32[]{:S(2)}) copy-start(bf16[4096,16]{0,1:T(8,128)(2,1)} %param.34) | copy-start | bytes 393220
  258.9 6.6 %copy-start.1 = (f32[2,65536]{1,0:T(2,128)S(1)}, f32[2,65536]{1,0:T(2,128)}, u32[]{:S(2)}) copy-start(f32[2,65536]{1,0:T(2,128)} %param.27) | copy-start | bytes 1572868
Sparse Core Ops, SparseCore 0:
  9.7 42.8 all-gather.2
  101.4 46.4 all-gather.4
  175.9 52.6 reduce-scatter.1
where the time goes:
time: 273 us; the launch traced here: 272 us
  waiting for transfers between devices  118 us (43%)
  local copies, waits for them, and re-layouts  40.1 us (15%)
  matrix products  39.5 us (14%)
  blocking collectives  23.7 us (9%)
  starting transfers between devices  17.5 us (6%)
  other arithmetic  17.4 us (6%)
  between operations  16.2 us (6%)
    reduce_scatter x1, waiting for transfers between devices, local(): lax.psum_scatter(apply_expert(gathered, up_local, down_local).astype(jnp....  51.6 us
    all_gather x1, waiting for transfers between devices, local(): gathered = lax.all_gather(received, 'dp', axis=0, tiled=True)  46.6 us
    all_to_all x1, blocking collectives, local(): lax.all_to_all(dispatch, 'expert', split_axis=0, concat_axis=0, tiled=True)  23.7 us
    dot_general x1, matrix products, apply_expert(): jnp.dot(hidden, down_local, preferred_element_type=jnp.float32)  14.1 us
    all_to_all x1, waiting for transfers between devices, local(): lax.all_to_all(sent_states.astype(jnp.bfloat16), 'dp', split_axis=0, conc...  14.1 us
    dot_general x1, matrix products, apply_expert(): jnp.dot(flattened, up_local, preferred_element_type=jnp.float32)  13.7 us
    unnamed x37, local copies, waits for them, and re-layouts  8.46 us
    all_to_all x1, starting transfers between devices, local(): lax.all_to_all(own_sums.astype(jnp.bfloat16), 'expert', split_axis=0, con...  6.87 us
  transfers between devices with their start and end apart: 6, of which 4 were waited for; matrix products, arithmetic and copies ran while one was open for 16% of the time, Pallas kernels for 0%

commit v1 on v0

v1 whole, which is shorter than its diff:
```python
import jax
import jax.numpy as jnp
from jax import lax
from jax.experimental import pallas as pl
from jax.experimental.pallas import tpu as pltpu
from jax.sharding import PartitionSpec as P

HEADS = 32
KV_HEADS = 8
HEAD = 128
SSM_DIM = 64
NSTATE = 16
BLOCK = 16
CAP = 8
MESH = pl.DeviceIdType.MESH
F32 = jnp.float32
BF16 = jnp.bfloat16


def dot(a, b, dims=((1,), (0,)), precision=None):
    return lax.dot_general(a, b, (dims, ((), ())), precision=precision, preferred_element_type=F32)


def split(x):
    high = x.astype(BF16)
    return high, (x - high.astype(F32)).astype(BF16)


def iota(shape, axis):
    return lax.broadcasted_iota(jnp.int32, shape, axis)


def position():
    me = lax.axis_index("dp")
    chips = lax.axis_size("dp") // 2
    z, core = me // 2, lax.rem(me, 2)
    up = lax.rem(z + 1, chips) * 2 + core
    down = lax.rem(z + chips - 1, chips) * 2 + core
    pair = z * 2 + 1 - core
    return z, core, lax.axis_index("expert"), up, down, pair


class Copies:
    def __init__(self, send, recv):
        self.send, self.recv, self.made = send, recv, []

    def start(self, source, target, device):
        at = len(self.made)
        copy = pltpu.make_async_remote_copy(
            src_ref=source,
            dst_ref=target,
            send_sem=self.send.at[at],
            recv_sem=self.recv.at[at],
            device_id=device,
            device_id_type=MESH,
        )
        copy.start()
        self.made.append(copy)
        return copy

    def finish(self):
        for copy in self.made:
            copy.wait_send()


FRONT_COPIES = 22


def front_kernel(
    holder_ref,
    index_ref,
    count_ref,
    owner_ref,
    state_row_ref,
    tokens_ref,
    queries_ref,
    kv_ref,
    x_ref,
    maps_ref,
    step_ref,
    decay_ref,
    pool_ref,
    states_ref,
    gain_ref,
    router_ref,
    ids_ref,
    rows_ref,
    mixed_ref,
    gates_ref,
    final_ref,
    pools,
    starts,
    keys,
    wide,
    send,
    recv,
    local,
):
    z, core, column, up, down, pair = position()
    barrier = pltpu.get_barrier_semaphore()
    for peer in (pair, up, down):
        pl.semaphore_signal(barrier, inc=1, device_id=(peer, column), device_id_type=MESH)
    pl.semaphore_wait(barrier, 3)

    copies = Copies(send, recv)
    half = pool_ref.shape[0] // 2
    first, second = pl.ds(0, half), pl.ds(half, half)
    kinds = ((pool_ref, pools, first, second), (states_ref, starts, pl.ds(0, 1), pl.ds(1, 1)))
    to_up, to_down, shared = [], [], []
    for mine, store, low, high in kinds:
        to_up.append(copies.start(mine.at[low], store.at[3, 0, low], (up, column)))
        to_down.append(copies.start(mine.at[high], store.at[1, 0, high], (down, column)))
    for mine, store, low, high in kinds:
        to_up.append(copies.start(mine.at[high], store.at[3, 0, high], (up, column)))
        to_down.append(copies.start(mine.at[low], store.at[1, 0, low], (down, column)))
    own = []
    for n, (mine, store, low, high) in enumerate(kinds):
        shared.append(copies.start(mine, store.at[0, 1], (pair, column)))
        copy = pltpu.make_async_copy(mine, store.at[0, 0], local.at[n])
        copy.start()
        own.append(copy)

    length = tokens_ref.shape[0]
    width = tokens_ref.shape[1]
    groups = HEADS // KV_HEADS
    span = groups * HEAD
    past = keys.shape[0] - length
    entries = past // BLOCK

    ones = (iota((length, length), 0) >= iota((length, length), 1)).astype(F32)
    running = dot(ones, decay_ref[...], precision=lax.Precision.HIGHEST)
    fade = jnp.concatenate(split(jnp.exp(running)), 1)
    lift = jnp.concatenate(split(jnp.exp(-running) * step_ref[...]), 1)
    entry_maps = maps_ref[:NSTATE]
    readout = maps_ref[NSTATE:]
    inter = dot(readout, entry_maps, ((0,), (0,)), lax.Precision.HIGHEST)
    inter = jnp.where(ones > 0.5, inter, 0.0).astype(BF16)
    entry16 = entry_maps.astype(BF16)
    readout16 = readout.astype(BF16)

    ids = ids_ref[...]
    experts = router_ref.shape[0]
    hot = [(iota((experts, length), 0) == ids[j : j + 1]).astype(F32) for j in (0, 1)]
    earlier = (iota((length, length), 0) < iota((length, length), 1)).astype(F32)
    before = dot(hot[0] + hot[1], earlier)
    slots = [jnp.sum(before * h, axis=0, keepdims=True) for h in hot]
    targets = [ids[j : j + 1] * CAP + slots[j].astype(jnp.int32) for j in (0, 1)]
    picks = [(iota((experts * CAP, length), 0) == t).astype(F32) for t in targets]

    to_up[0].wait_recv()
    to_up[1].wait_recv()
    passed = []
    for mine, store, low, high in kinds:
        passed.append(copies.start(store.at[3, 0, low], store.at[2, 0, low], (up, column)))
    to_down[0].wait_recv()
    to_down[1].wait_recv()
    for mine, store, low, high in kinds:
        passed.append(copies.start(store.at[1, 0, high], store.at[2, 0, high], (down, column)))
    to_up[2].wait_recv()
    to_up[3].wait_recv()
    for mine, store, low, high in kinds:
        shared.append(copies.start(store.at[3, 0], store.at[3, 1], (pair, column)))
    to_down[2].wait_recv()
    to_down[3].wait_recv()
    for mine, store, low, high in kinds:
        shared.append(copies.start(store.at[1, 0], store.at[1, 1], (pair, column)))
    for copy in passed:
        copy.wait_recv()
    for mine, store, low, high in kinds:
        shared.append(copies.start(store.at[2, 0, low], store.at[2, 1, low], (pair, column)))
        shared.append(copies.start(store.at[2, 0, high], store.at[2, 1, high], (pair, column)))
    for copy in own:
        copy.wait()
    for copy in shared:
        copy.wait_recv()

    chips = lax.axis_size("dp") // 2

    def place(holder):
        return lax.rem(lax.div(holder, 2) - z + chips, chips), lax.rem(lax.rem(holder, 2) + core, 2)

    for entry in range(entries):
        ring, side = place(holder_ref[entry])
        keys[pl.ds(entry * BLOCK, BLOCK), :] = pools[ring, side, index_ref[entry]]
    keys[pl.ds(past, length), :] = kv_ref[...]
    ring, side = place(owner_ref[0])
    state_row = state_row_ref[0]

    spots = iota((length, past + length), 1)
    cached = count_ref[0] * BLOCK
    bound = jnp.where(spots < past, cached, past + 1 + iota((length, past + length), 0))
    bias = jnp.where(spots < bound, 0.0, -jnp.inf)
    bias = jnp.concatenate([bias] * groups, 0)
    kv_width = KV_HEADS * HEAD

    def chunk(g, total):
        lanes = pl.ds(pl.multiple_of(g * span, span), span)
        query = queries_ref[:, lanes]
        query = jnp.concatenate([query[:, j * HEAD : (j + 1) * HEAD] for j in range(groups)], 0)
        key = keys[:, pl.ds(pl.multiple_of(g * HEAD, HEAD), HEAD)]
        value = keys[:, pl.ds(pl.multiple_of(kv_width + g * HEAD, HEAD), HEAD)]
        scores = dot(query, key, ((1,), (1,))) * HEAD ** (-0.5) + bias
        weights = jnp.exp(scores - jnp.max(scores, axis=1, keepdims=True))
        weights = (weights / jnp.sum(weights, axis=1, keepdims=True)).astype(BF16)
        attended = dot(weights, value)
        attended = jnp.concatenate([attended[j * length : (j + 1) * length] for j in range(groups)], 1)

        heads = decay_ref.shape[1]
        head = iota((2 * heads, span), 0)
        head = jnp.where(head < heads, head, head - heads)
        owner = g * (span // SSM_DIM) + iota((2 * heads, span), 1) // SSM_DIM
        spread = (head == owner).astype(F32).astype(BF16)
        fading = dot(fade, spread)
        lifted = (dot(lift, spread) * x_ref[:, lanes].astype(F32)).astype(BF16)
        start = starts[ring, side, state_row, :, lanes]
        scanned = fading * (dot(inter, lifted) + dot(readout16, start, ((0,), (0,))))
        final_ref[:, lanes] = fading[length - 1 : length] * (dot(entry16, lifted) + start.astype(F32))
        mixed = (tokens_ref[:, lanes].astype(F32) + (attended + scanned)).astype(BF16)
        mixed_ref[:, lanes] = mixed
        mixed = mixed.astype(F32)
        wide[:, lanes] = mixed
        return total + jnp.sum(mixed * mixed, axis=1, keepdims=True)

    total = lax.fori_loop(0, width // span, chunk, jnp.zeros((length, 1), F32))
    scale = lax.rsqrt(total / width + 1e-05)
    pick = (picks[0] + picks[1]).astype(BF16)

    def send_rows(g, logits):
        lanes = pl.ds(pl.multiple_of(g * span, span), span)
        normed = (wide[:, lanes] * scale * gain_ref[:, lanes]).astype(BF16)
        rows_ref[:, lanes] = dot(pick, normed).astype(BF16)
        return logits + dot(router_ref[:, lanes], normed, ((1,), (1,)))

    logits = lax.fori_loop(0, width // span, send_rows, jnp.zeros((experts, length), F32))
    chosen = [jnp.sum(logits * h, axis=0, keepdims=True) for h in hot]
    lifted = [1.0 / (1.0 + jnp.exp(-v)) for v in chosen]
    both = lifted[0] + lifted[1]
    gates_ref[...] = picks[0] * (lifted[0] / both) + picks[1] * (lifted[1] / both)
    copies.finish()


def expert_kernel(
    rows_ref,
    mixed_ref,
    gates_ref,
    up_ref,
    down_ref,
    out_ref,
    up_w,
    down_w,
    x,
    sums,
    hidden,
    mine,
    theirs,
    others,
    relay,
    ring,
    owned,
    back,
    send,
    recv,
    local,
):
    z, core, column, up, down, pair = position()
    me = lax.axis_index("dp")
    columns = lax.axis_size("expert")
    loads = [
        pltpu.make_async_copy(up_ref.at[0], up_w, local.at[0]),
        pltpu.make_async_copy(down_ref.at[0], down_w, local.at[1]),
    ]
    for load in loads:
        load.start()
    barrier = pltpu.get_barrier_semaphore()
    for k in range(1, columns):
        pl.semaphore_signal(
            barrier, inc=1, device_id=(me, lax.rem(column + k, columns)), device_id_type=MESH
        )
    for peer in (pair, up, down):
        pl.semaphore_signal(barrier, inc=1, device_id=(peer, column), device_id_type=MESH)
    pl.semaphore_wait(barrier, columns + 2)

    copies = Copies(send, recv)

    def rows_of(peer):
        return pl.ds(pl.multiple_of(peer * CAP, CAP), CAP)

    keep = pltpu.make_async_copy(rows_ref.at[rows_of(column)], x.at[0, 0, rows_of(column)], local.at[2])
    keep.start()
    dealt = []
    for k in range(1, columns):
        peer = lax.rem(column + k, columns)
        dealt.append(copies.start(rows_ref.at[rows_of(peer)], x.at[0, 0, rows_of(column)], (me, peer)))
    keep.wait()
    for copy in dealt:
        copy.wait_recv()

    half = x.shape[2] // 2
    low, high = pl.ds(0, half), pl.ds(half, half)
    width = x.shape[3]
    up_low = copies.start(x.at[0, 0, low], x.at[3, 0, low], (up, column))
    down_high = copies.start(x.at[0, 0, high], x.at[1, 0, high], (down, column))
    up_high = copies.start(x.at[0, 0, high], x.at[3, 0, high], (up, column))
    down_low = copies.start(x.at[0, 0, low], x.at[1, 0, low], (down, column))
    shared = copies.start(x.at[0, 0], x.at[0, 1], (pair, column))

    tile = 512

    def multiply(k):
        sums[...] = jnp.zeros_like(sums)

        def grow(i, carry):
            lanes = pl.ds(pl.multiple_of(i * tile, tile), tile)
            left = jnp.concatenate([x[k, 0, :, lanes], x[k, 1, :, lanes]], 0)
            sums[...] += dot(left, up_w[lanes, :])
            return carry

        lax.fori_loop(0, width // tile, grow, 0)
        total = sums[...]
        hidden[...] = (total / (1.0 + jnp.exp(-total))).astype(BF16)

        def shrink(i, carry):
            lanes = pl.ds(pl.multiple_of(i * tile, tile), tile)
            part = dot(hidden[...], down_w[:, lanes]).astype(BF16)
            mine[k, :, lanes] = part[: 2 * half]
            theirs[k, :, lanes] = part[2 * half :]
            return carry

        lax.fori_loop(0, width // tile, shrink, 0)

    def give(k):
        return copies.start(theirs.at[k], others.at[k], (pair, column))

    def add(target, spot, *terms):
        def piece(i, carry):
            lanes = pl.ds(pl.multiple_of(i * tile, tile), tile)
            total = terms[0][0][terms[0][1] + (lanes,)].astype(F32)
            for ref, at in terms[1:]:
                total += ref[at + (lanes,)].astype(F32)
            target[spot + (lanes,)] = total.astype(BF16)
            return carry

        lax.fori_loop(0, width // tile, piece, 0)

    up_low.wait_recv()
    pass_up = copies.start(x.at[3, 0, low], x.at[2, 0, low], (up, column))
    down_high.wait_recv()
    pass_down = copies.start(x.at[1, 0, high], x.at[2, 0, high], (down, column))
    shared.wait_recv()
    for load in loads:
        load.wait()
    multiply(0)
    given0 = give(0)
    up_high.wait_recv()
    share3 = copies.start(x.at[3, 0], x.at[3, 1], (pair, column))
    down_low.wait_recv()
    share1 = copies.start(x.at[1, 0], x.at[1, 1], (pair, column))
    share3.wait_recv()
    multiply(3)
    given3 = give(3)
    share1.wait_recv()
    multiply(1)
    given1 = give(1)
    pass_up.wait_recv()
    share_low = copies.start(x.at[2, 0, low], x.at[2, 1, low], (pair, column))
    pass_down.wait_recv()
    share_high = copies.start(x.at[2, 0, high], x.at[2, 1, high], (pair, column))
    given1.wait_recv()
    given3.wait_recv()
    add(mine, (1, high), (mine, (1, high)), (others, (1, high)))
    sent1 = copies.start(mine.at[1, high], ring.at[0, high], (up, column))
    add(mine, (3, low), (mine, (3, low)), (others, (3, low)))
    sent3 = copies.start(mine.at[3, low], ring.at[1, low], (down, column))
    share_low.wait_recv()
    share_high.wait_recv()
    multiply(2)
    given2 = give(2)
    given2.wait_recv()
    add(mine, (2, low), (mine, (2, low)), (others, (2, low)))
    relay_up = copies.start(mine.at[2, low], relay.at[0], (up, column))
    add(mine, (2, high), (mine, (2, high)), (others, (2, high)))
    relay_down = copies.start(mine.at[2, high], relay.at[1], (down, column))
    given0.wait_recv()
    every = pl.ds(0, 2 * half)
    add(mine, (0, every), (mine, (0, every)), (others, (0, every)))
    relay_up.wait_recv()
    add(mine, (1, low), (mine, (1, low)), (others, (1, low)), (relay, (0, low)))
    last1 = copies.start(mine.at[1, low], ring.at[0, low], (up, column))
    relay_down.wait_recv()
    add(mine, (3, high), (mine, (3, high)), (others, (3, high)), (relay, (1, low)))
    last3 = copies.start(mine.at[3, high], ring.at[1, high], (down, column))
    for copy in (sent1, sent3, last1, last3):
        copy.wait_recv()
    add(owned, (every,), (mine, (0, every)), (ring, (0, every)), (ring, (1, every)))

    keep = pltpu.make_async_copy(owned.at[rows_of(column)], back.at[rows_of(column)], local.at[3])
    keep.start()
    returned = []
    for k in range(1, columns):
        peer = lax.rem(column + k, columns)
        returned.append(copies.start(owned.at[rows_of(peer)], back.at[rows_of(column)], (me, peer)))
    weight_high, weight_low = split(gates_ref[...])
    keep.wait()
    for copy in returned:
        copy.wait_recv()

    def combine(i, carry):
        lanes = pl.ds(pl.multiple_of(i * tile, tile), tile)
        rows = back[:, lanes]
        total = dot(weight_high, rows, ((0,), (0,))) + dot(weight_low, rows, ((0,), (0,)))
        out_ref[:, lanes] = (mixed_ref[:, lanes].astype(F32) + total).astype(BF16)
        return carry

    lax.fori_loop(0, width // tile, combine, 0)
    copies.finish()


EXPERT_COPIES = 2 * 15 + 5 + 2 + 4 + 4 + 2 + 2 + 2


def local(
    tokens,
    queries,
    keys_values,
    scan_input,
    state_maps,
    step_size,
    step_decay,
    block_pool,
    state_pool,
    block_holder,
    block_index,
    cached_blocks,
    state_holder,
    state_index,
    norm_gain,
    router_weight,
    expert_ids,
    up_weight,
    down_weight,
):
    length, width = tokens.shape
    experts = router_weight.shape[1]
    chips = lax.axis_size("dp") // 2
    pool_rows, state_rows = block_pool.shape[0], state_pool.shape[0]
    entries = block_holder.shape[1]
    kv = keys_values.shape[1]
    states = state_pool.reshape(state_rows, -1, NSTATE).astype(BF16).transpose(0, 2, 1)
    smem = pl.BlockSpec(memory_space=pltpu.SMEM)
    vmem = pl.BlockSpec(memory_space=pltpu.VMEM)
    anywhere = pl.BlockSpec(memory_space=pl.ANY)
    dma = pltpu.SemaphoreType.DMA
    rows, mixed, gates, final = pl.pallas_call(
        front_kernel,
        out_shape=(
            jax.ShapeDtypeStruct((experts * CAP, width), BF16),
            jax.ShapeDtypeStruct((length, width), BF16),
            jax.ShapeDtypeStruct((experts * CAP, length), F32),
            jax.ShapeDtypeStruct((NSTATE, width), F32),
        ),
        in_specs=[smem] * 5 + [vmem] * 12,
        out_specs=(vmem,) * 4,
        scratch_shapes=[
            pltpu.VMEM((chips, 2, pool_rows, BLOCK, kv), BF16),
            pltpu.VMEM((chips, 2, state_rows, NSTATE, width), BF16),
            pltpu.VMEM((entries * BLOCK + length, kv), BF16),
            pltpu.VMEM((length, width), F32),
            dma((FRONT_COPIES,)),
            dma((FRONT_COPIES,)),
            dma((2,)),
        ],
        compiler_params=pltpu.CompilerParams(
            collective_id=0, has_side_effects=True, vmem_limit_bytes=40 << 20
        ),
        name="front",
    )(
        block_holder[0],
        block_index[0],
        cached_blocks,
        state_holder,
        state_index,
        tokens,
        queries,
        keys_values,
        scan_input,
        state_maps.T,
        step_size,
        step_decay,
        block_pool,
        states,
        norm_gain[None, :],
        router_weight.T,
        expert_ids.T,
    )
    hidden = up_weight.shape[2]
    count = experts * CAP
    layer_out = pl.pallas_call(
        expert_kernel,
        out_shape=jax.ShapeDtypeStruct((length, width), BF16),
        in_specs=[vmem] * 3 + [anywhere] * 2,
        out_specs=vmem,
        scratch_shapes=[
            pltpu.VMEM((width, hidden), BF16),
            pltpu.VMEM((hidden, width), BF16),
            pltpu.VMEM((chips, 2, count, width), BF16),
            pltpu.VMEM((2 * count, hidden), F32),
            pltpu.VMEM((2 * count, hidden), BF16),
            pltpu.VMEM((chips, count, width), BF16),
            pltpu.VMEM((chips, count, width), BF16),
            pltpu.VMEM((chips, count, width), BF16),
            pltpu.VMEM((2, count // 2, width), BF16),
            pltpu.VMEM((2, count, width), BF16),
            pltpu.VMEM((count, width), BF16),
            pltpu.VMEM((count, width), BF16),
            dma((EXPERT_COPIES,)),
            dma((EXPERT_COPIES,)),
            dma((4,)),
        ],
        compiler_params=pltpu.CompilerParams(
            collective_id=1, has_side_effects=True, vmem_limit_bytes=58 << 20
        ),
        name="experts",
    )(rows, mixed, gates, up_weight, down_weight)
    return (layer_out, final.T.reshape(1, -1))


def solution(mesh):
    placed = (
        P(("dp", "expert"), None),
        P(("dp", "expert"), None),
        P(("dp", "expert"), None),
        P(("dp", "expert"), None),
        P(("dp", "expert"), None),
        P(("dp", "expert"), None),
        P(("dp", "expert"), None),
        P(("dp", "expert"), None, None),
        P(("dp", "expert"), None),
        P(("dp", "expert"), None),
        P(("dp", "expert"), None),
        P(("dp", "expert")),
        P(("dp", "expert")),
        P(("dp", "expert")),
        P(),
        P(),
        P(("dp", "expert"), None),
        P("expert", None, "dp"),
        P("expert", "dp", None),
    )
    return jax.shard_map(
        local,
        mesh=mesh,
        in_specs=placed,
        out_specs=(P(("dp", "expert"), None), P(("dp", "expert"), None)),
        check_vma=False,
    )
```

time: 273 us -> 193 us (0.71)
  Pallas kernels: 0 us -> 167 us
  waiting for transfers between devices: 118 us -> 0 us
  matrix products: 39.5 us -> 0 us
  blocking collectives: 23.7 us -> 0 us
  local copies, waits for them, and re-layouts: 40.1 us -> 19.6 us
  starting transfers between devices: 17.5 us -> 0 us
  other arithmetic: 17.4 us -> 1.22 us
  between operations: 16.2 us -> 2.64 us
    pallas_call x0 -> x2, Pallas kernels: none -> 167 us  [the longest x1 126 us: local(): pl.pallas_call(expert_kernel, out_shape=jax.ShapeDtypeStruct((length, wid...]
    reduce_scatter x1 -> x0, waiting for transfers between devices: 51.6 us -> none  [local(): lax.psum_scatter(apply_expert(gathered, up_local, down_local).astype(jnp....]
    all_gather x2 -> x0, waiting for transfers between devices: 46.6 us -> none  [the longest x1 46.6 us: local(): gathered = lax.all_gather(received, 'dp', axis=0, tiled=True)]
    dot_general x9 -> x0, matrix products: 39.5 us -> none  [the longest x1 14.1 us: apply_expert(): jnp.dot(hidden, down_local, preferred_element_type=jnp.float32)]
    all_to_all x1 -> x0, blocking collectives: 23.7 us -> none  [local(): lax.all_to_all(dispatch, 'expert', split_axis=0, concat_axis=0, tiled=True)]
    all_to_all x3 -> x0, waiting for transfers between devices: 18.9 us -> none  [the longest x1 14.1 us: local(): lax.all_to_all(sent_states.astype(jnp.bfloat16), 'dp', split_axis=0, conc...]
    all_to_all x3 -> x0, starting transfers between devices: 17.2 us -> none  [the longest x1 6.87 us: local(): lax.all_to_all(own_sums.astype(jnp.bfloat16), 'expert', split_axis=0, con...]
    gather x9 -> x0, local copies, waits for them, and re-layouts: 9.81 us -> none  [the longest x1 2.92 us: local(): prefix = pooled[row_ids]]
  transfers between devices with their start and end apart: 6 -> 0, of which waited for: 4 -> 0; matrix products, arithmetic and copies ran while one was open for 16% -> 0% of each run, Pallas kernels for 0% -> 0%
where the time goes in v1:
time: 193 us; the launch traced here: 191 us
  Pallas kernels  167 us (87%)
  local copies, waits for them, and re-layouts  19.6 us (10%)
  between operations  2.64 us (1%)
    pallas_call x1, Pallas kernels, local(): pl.pallas_call(expert_kernel, out_shape=jax.ShapeDtypeStruct((length, wid...  126 us
    pallas_call x1, Pallas kernels, local(): pl.pallas_call(front_kernel, out_shape=(jax.ShapeDtypeStruct((experts * C...  41.6 us
    unnamed x33, local copies, waits for them, and re-layouts  15.2 us

profile of v1, /device:TPU:0, one launch (start us, length us, event | category | flops | bytes accessed | tf_op | source)
XLA Modules:
  0.0 190.8 jit_solution(2945042566870673136)
XLA Ops:
  2.6 1.2 convert_element_type.6
  3.8 1.5 convert_element_type.7
  5.3 0.8 copy.21
  6.1 0.0 copy-start.1
  6.1 1.0 copy-done.1
  7.1 0.0 copy-start.2
  7.1 1.0 copy-done.2
  8.2 0.0 copy-start.3
  8.2 1.0 copy-done.3
  9.2 0.0 copy-start.4
  9.2 1.0 copy-done.4
  10.3 0.0 copy-start.6
  10.3 0.9 copy-done.6
  11.2 0.0 copy-start.7
  11.2 0.9 copy-done.7
  12.1 0.0 copy-start.9
  12.1 0.8 copy-done.9
  12.9 0.0 copy-start.10
  12.9 0.8 copy-done.10
  13.6 0.0 copy-start.11
  13.6 0.7 copy-done.11
  14.4 0.0 copy-start.12
  14.4 0.7 copy-done.12
  15.1 0.0 copy-start.13
  15.1 0.7 copy-done.13
  15.8 0.0 copy-start.14
  15.8 0.7 copy-done.14
  16.4 0.0 copy-start.15
  16.4 0.7 copy-done.15
  17.1 41.6 %front.1 = (bf16[128,4096]{1,0:T(8,128)(2,1)S(1)}, bf16[64,4096]{1,0:T(8,128)(2,1)S(1)}, f32[128,64]{1,0:T(8,128)S(1)}, f32[16,4096]{1,0:T(8,128)S(1)}) custom-call(s32[16]{0:T(128)S(1)} %bitcast.14, s32[16]{0:T(128)S(1)} %bitcast.15, s32[1]{0:T(128)S(6)} %copy.24.count_ref, s32[1]{0:T(128)S(6)} %copy.25.owner_ref, s32[1]{0:T(128)S(6)} %copy.26.state_row_ref, ...), custom_call_target="tpu_custom_call" | custom-call | tf_op jit(solution)/shard_map/front/pallas_call | solution.py:453
  58.7 0.0 copy-start
  58.7 1.0 copy-done
  59.7 0.0 copy-start.5
  59.7 0.8 copy-done.5
  60.5 0.0 copy-start.8
  60.5 0.6 copy-done.8
  61.1 125.7 %experts.1 = bf16[64,4096]{1,0:T(8,128)(2,1)} custom-call(bf16[128,4096]{1,0:T(8,128)(2,1)} %copy-done, bf16[64,4096]{1,0:T(8,128)(2,1)} %copy-done.5, f32[128,64]{1,0:T(8,128)} %copy-done.8, bf16[1,4096,896]{2,1,0:T(8,128)(2,1)} %up_ref.1, bf16[1,896,4096]{2,1,0:T(8,128)(2,1)} %down_ref.1), custom_call_target="tpu_custom_call" | custom-call | tf_op jit(solution)/shard_map/experts/pallas_call | solution.py:497
  186.9 0.6 copy.22
  187.5 1.5 reshape.9
  188.9 1.9 copy.27
Async XLA Ops:
  6.1 1.0 copy-start.1
  7.1 1.0 copy-start.2
  8.2 1.0 copy-start.3
  9.2 1.0 copy-start.4
  10.3 0.9 copy-start.6
  11.2 0.9 copy-start.7
  12.1 0.8 copy-start.9
  12.9 0.8 copy-start.10
  13.6 0.7 copy-start.11
  14.4 0.7 copy-start.12
  15.1 0.7 copy-start.13
  15.8 0.7 copy-start.14
  16.4 0.7 copy-start.15
  58.7 1.0 copy-start
  59.7 0.8 copy-start.5
  60.5 0.6 copy-start.8

commit v2 on v0

v2 whole, which is shorter than its diff:
```python
import jax
import jax.numpy as jnp
from jax import lax
from jax.experimental import pallas as pl
from jax.experimental.pallas import tpu as pltpu
from jax.sharding import PartitionSpec as P

HEADS = 32
KV_HEADS = 8
HEAD = 128
SSM_DIM = 64
NSTATE = 16
BLOCK = 16
CAP = 8
MESH = pl.DeviceIdType.MESH
F32 = jnp.float32
BF16 = jnp.bfloat16


def dot(a, b, dims=((1,), (0,)), precision=None):
    return lax.dot_general(a, b, (dims, ((), ())), precision=precision, preferred_element_type=F32)


def split(x):
    high = x.astype(BF16)
    return high, (x - high.astype(F32)).astype(BF16)


def iota(shape, axis):
    return lax.broadcasted_iota(jnp.int32, shape, axis)


def position():
    me = lax.axis_index("dp")
    chips = lax.axis_size("dp") // 2
    z, core = me // 2, lax.rem(me, 2)
    up = lax.rem(z + 1, chips) * 2 + core
    down = lax.rem(z + chips - 1, chips) * 2 + core
    pair = z * 2 + 1 - core
    return z, core, lax.axis_index("expert"), up, down, pair


class Copies:
    def __init__(self, send, recv):
        self.send, self.recv, self.made = send, recv, []

    def start(self, source, target, device):
        at = len(self.made)
        copy = pltpu.make_async_remote_copy(
            src_ref=source,
            dst_ref=target,
            send_sem=self.send.at[at],
            recv_sem=self.recv.at[at],
            device_id=device,
            device_id_type=MESH,
        )
        copy.start()
        self.made.append(copy)
        return copy

    def finish(self):
        for copy in self.made:
            copy.wait_send()


GROUPS = 2


def layer_kernel(
    holder_hbm,
    index_hbm,
    count_hbm,
    owner_hbm,
    state_row_hbm,
    tokens_hbm,
    queries_hbm,
    kv_hbm,
    x_hbm,
    maps_hbm,
    step_hbm,
    decay_hbm,
    pool_hbm,
    states_hbm,
    gain_hbm,
    router_hbm,
    ids_hbm,
    up_ref,
    down_ref,
    out_ref,
    final_ref,
    holder_ref,
    index_ref,
    count_ref,
    owner_ref,
    state_row_ref,
    tokens_ref,
    queries_ref,
    x_ref,
    maps_ref,
    step_ref,
    decay_ref,
    gain_ref,
    router_ref,
    ids_ref,
    states_ref,
    pools,
    starts,
    keys,
    wide,
    mixed_ref,
    rows_ref,
    up_w,
    down_w,
    x,
    sums,
    hidden,
    mine,
    theirs,
    others,
    relay,
    ring,
    owned,
    back,
    send,
    recv,
    dealt,
    returned,
    local,
):
    z, core, column, up, down, pair = position()
    me = lax.axis_index("dp")
    columns = lax.axis_size("expert")
    chips = lax.axis_size("dp") // 2
    length, width = tokens_ref.shape
    groups = HEADS // KV_HEADS
    span = groups * HEAD
    past = keys.shape[0] - length
    entries = past // BLOCK

    barrier = pltpu.get_barrier_semaphore()
    for k in range(1, columns):
        pl.semaphore_signal(
            barrier, inc=1, device_id=(me, lax.rem(column + k, columns)), device_id_type=MESH
        )
    for peer in (pair, up, down):
        pl.semaphore_signal(barrier, inc=1, device_id=(peer, column), device_id_type=MESH)

    fetched = (
        (pool_hbm, pools.at[0, 0]),
        (states_hbm, states_ref),
        (decay_hbm, decay_ref),
        (step_hbm, step_ref),
        (maps_hbm, maps_ref),
        (x_hbm, x_ref),
        (ids_hbm, ids_ref),
        (holder_hbm, holder_ref),
        (index_hbm, index_ref),
        (count_hbm, count_ref),
        (owner_hbm, owner_ref),
        (state_row_hbm, state_row_ref),
        (queries_hbm, queries_ref),
        (kv_hbm, keys.at[pl.ds(past, length)]),
        (tokens_hbm, tokens_ref),
        (gain_hbm, gain_ref),
        (router_hbm, router_ref),
        (up_ref.at[0], up_w),
        (down_ref.at[0], down_w),
    )
    loads = [pltpu.make_async_copy(a, b, local.at[n]) for n, (a, b) in enumerate(fetched)]
    for load in loads[:-2]:
        load.start()

    pl.semaphore_wait(barrier, columns + 2)

    copies = Copies(send, recv)
    half = pools.shape[2] // 2
    first, second = pl.ds(0, half), pl.ds(half, half)
    kinds = (
        (pools.at[0, 0], pools, first, second),
        (starts.at[0, 0], starts, pl.ds(0, 1), pl.ds(1, 1)),
    )
    loads[0].wait()
    loads[1].wait()
    for n in range(states_ref.shape[1]):
        starts[0, 0, n] = states_ref[:, n, :].astype(BF16)
    to_up, to_down, shared = [], [], []
    for own, store, low, high in kinds:
        to_up.append(copies.start(own.at[low], store.at[3, 0, low], (up, column)))
        to_down.append(copies.start(own.at[high], store.at[1, 0, high], (down, column)))
    for own, store, low, high in kinds:
        to_up.append(copies.start(own.at[high], store.at[3, 0, high], (up, column)))
        to_down.append(copies.start(own.at[low], store.at[1, 0, low], (down, column)))
    for own, store, low, high in kinds:
        shared.append(copies.start(own, store.at[0, 1], (pair, column)))

    for load in loads[2:7]:
        load.wait()
    heads = decay_ref.shape[1]
    ones = (iota((length, length), 0) >= iota((length, length), 1)).astype(F32)
    running = dot(ones, decay_ref[...], precision=lax.Precision.HIGHEST)
    decayed = jnp.exp(running)
    fade = jnp.concatenate(split(decayed), 1)
    lift = jnp.concatenate(split(jnp.exp(-running) * step_ref[...]), 1)
    entry_maps = maps_ref[:NSTATE]
    readout = maps_ref[NSTATE:]
    inter = dot(readout, entry_maps, ((0,), (0,)), lax.Precision.HIGHEST)
    inter = jnp.where(ones > 0.5, inter, 0.0).astype(BF16)
    packed = 128 // NSTATE
    depth = span // packed
    repeat = (lax.rem(iota((NSTATE, 128), 1), NSTATE) == iota((NSTATE, 128), 0)).astype(F32).astype(BF16)
    entry_rows = dot(entry_maps.astype(BF16), repeat, ((0,), (0,))).astype(BF16)
    readout_rows = dot(readout.astype(BF16), repeat, ((0,), (0,))).astype(BF16)
    unpack = (iota((span, depth), 0) // packed == iota((span, depth), 1)).astype(F32).astype(BF16)
    lane_kept = (iota((span, 128), 1) // NSTATE == lax.rem(iota((span, 128), 0), packed)).astype(F32)

    ids = ids_ref[...]
    experts = router_ref.shape[0]
    hot = [(iota((experts, length), 0) == ids[j : j + 1]).astype(F32) for j in (0, 1)]
    earlier = (iota((length, length), 0) < iota((length, length), 1)).astype(F32)
    before = dot(hot[0] + hot[1], earlier)
    slots = [jnp.sum(before * h, axis=0, keepdims=True) for h in hot]
    targets = [ids[j : j + 1] * CAP + slots[j].astype(jnp.int32) for j in (0, 1)]
    picks = [(iota((experts * CAP, length), 0) == t).astype(F32) for t in targets]

    def spread_of(g):
        head = iota((2 * heads, span), 0)
        head = jnp.where(head < heads, head, head - heads)
        owner = g * (span // SSM_DIM) + iota((2 * heads, span), 1) // SSM_DIM
        return (head == owner).astype(F32).astype(BF16)

    def scan(g, carry):
        lanes = pl.ds(pl.multiple_of(g * span, span), span)
        spread = spread_of(g)
        lifted = (dot(lift, spread) * x_ref[:, lanes].astype(F32)).astype(BF16)
        wide[:, lanes] = dot(fade, spread) * dot(inter, lifted)
        added = dot(lifted, entry_rows, ((0,), (0,))) * lane_kept
        added = jnp.sum(added.reshape(depth, packed, 128), axis=1)
        final_ref[pl.ds(pl.multiple_of(g * depth, depth), depth), :] = added
        return carry

    lax.fori_loop(0, width // span, scan, 0)

    passed = []
    for n, (own, store, low, high) in enumerate(kinds):
        to_up[n].wait_recv()
        passed.append(copies.start(store.at[3, 0, low], store.at[2, 0, low], (up, column)))
        to_down[n].wait_recv()
        passed.append(copies.start(store.at[1, 0, high], store.at[2, 0, high], (down, column)))
    for n, (own, store, low, high) in enumerate(kinds):
        to_up[2 + n].wait_recv()
        shared.append(copies.start(store.at[3, 0], store.at[3, 1], (pair, column)))
        to_down[2 + n].wait_recv()
        shared.append(copies.start(store.at[1, 0], store.at[1, 1], (pair, column)))
    for n, (own, store, low, high) in enumerate(kinds):
        passed[2 * n].wait_recv()
        shared.append(copies.start(store.at[2, 0, low], store.at[2, 1, low], (pair, column)))
        passed[2 * n + 1].wait_recv()
        shared.append(copies.start(store.at[2, 0, high], store.at[2, 1, high], (pair, column)))
    for load in loads[7:-2]:
        load.wait()
    for copy in shared:
        copy.wait_recv()
    for load in loads[-2:]:
        load.start()

    def place(holder):
        return lax.rem(lax.div(holder, 2) - z + chips, chips), lax.rem(lax.rem(holder, 2) + core, 2)

    for entry in range(entries):
        side, other = place(holder_ref[0, entry])
        keys[pl.ds(entry * BLOCK, BLOCK), :] = pools[side, other, index_ref[0, entry]]
    side, other = place(owner_ref[0])
    state_row = state_row_ref[0]

    spots = iota((length, past + length), 1)
    cached = count_ref[0] * BLOCK
    bound = jnp.where(spots < past, cached, past + 1 + iota((length, past + length), 0))
    bias = jnp.where(spots < bound, 0.0, -jnp.inf)
    bias = jnp.concatenate([bias] * groups, 0)
    kv_width = KV_HEADS * HEAD
    ending = decayed[length - 1 : length]

    def chunk(g, total):
        lanes = pl.ds(g * span, span)
        query = queries_ref[:, lanes]
        query = jnp.concatenate([query[:, j * HEAD : (j + 1) * HEAD] for j in range(groups)], 0)
        key = keys[:, pl.ds(g * HEAD, HEAD)]
        value = keys[:, pl.ds(kv_width + g * HEAD, HEAD)]
        scores = dot(query, key, ((1,), (1,))) * HEAD ** (-0.5) + bias
        weights = jnp.exp(scores - jnp.max(scores, axis=1, keepdims=True))
        weights = (weights / jnp.sum(weights, axis=1, keepdims=True)).astype(BF16)
        attended = dot(weights, value)
        attended = jnp.concatenate([attended[j * length : (j + 1) * length] for j in range(groups)], 1)

        part = pl.ds(g * depth, depth)
        start = starts[side, other, state_row, part, :]
        channels = (dot(unpack, start) * lane_kept).astype(BF16)
        started = dot(readout_rows, channels, ((1,), (1,)))
        scanned = wide[:, lanes] + dot(fade, spread_of(g)) * started
        owner = g * (span // SSM_DIM) + iota((depth, heads), 0) // (SSM_DIM // packed)
        ended = jnp.sum(jnp.where(iota((depth, heads), 1) == owner, ending, 0.0), axis=1, keepdims=True)
        final_ref[part, :] = ended * (start.astype(F32) + final_ref[part, :])
        mixed = (tokens_ref[:, lanes].astype(F32) + (attended + scanned)).astype(BF16)
        mixed_ref[:, lanes] = mixed
        mixed = mixed.astype(F32)
        return total + jnp.sum(mixed * mixed, axis=1, keepdims=True)

    total = jnp.zeros((length, 1), F32)
    for g in range(width // span):
        total = chunk(g, total)
    scale = lax.rsqrt(total / width + 1e-05)
    pick = (picks[0] + picks[1]).astype(BF16)

    def dispatch(g, logits):
        lanes = pl.ds(g * span, span)
        normed = (mixed_ref[:, lanes].astype(F32) * scale * gain_ref[:, lanes]).astype(BF16)
        rows_ref[:, lanes] = dot(pick, normed).astype(BF16)
        return logits + dot(router_ref[:, lanes], normed, ((1,), (1,)))

    logits = jnp.zeros((experts, length), F32)
    for g in range(width // span):
        logits = dispatch(g, logits)

    side_len = 4
    share = columns // GROUPS * CAP
    row, place_in_row = column // side_len, lax.rem(column, side_len)
    offsets = [(k // side_len, k % side_len) for k in range(columns)]
    members = [[k for k, (a, b) in enumerate(offsets) if (a + b) % GROUPS == g] for g in range(GROUPS)]

    def at_offset(k):
        along, across = offsets[k]
        return lax.rem(row + along, side_len) * side_len + lax.rem(place_in_row + across, side_len)

    def from_offset(k):
        along, across = offsets[k]
        there = lax.rem(row + side_len - along, side_len)
        return there * side_len + lax.rem(place_in_row + side_len - across, side_len)

    def spot(g, source):
        return pl.ds(pl.multiple_of(g * share + source // GROUPS * CAP, CAP), CAP)

    def block(other):
        return pl.ds(pl.multiple_of(other * CAP, CAP), CAP)

    def dealing(g, k):
        peer = at_offset(k)
        return pltpu.make_async_remote_copy(
            src_ref=rows_ref.at[block(peer)],
            dst_ref=x.at[0, 0, spot(g, column)],
            send_sem=dealt.at[columns + k],
            recv_sem=dealt.at[k],
            device_id=(me, peer),
            device_id_type=MESH,
        )

    def deal(g):
        for k in members[g]:
            if k == 0:
                target = x.at[0, 0, spot(g, column)]
                pltpu.make_async_copy(rows_ref.at[block(column)], target, dealt.at[0]).start()
            else:
                dealing(g, k).start()

    def dealt_all(g):
        for k in members[g]:
            rows = x.at[0, 0, spot(g, from_offset(k))]
            pltpu.make_async_copy(rows, rows, dealt.at[k]).wait()

    def sending(g, k):
        peer = at_offset(k)
        return pltpu.make_async_remote_copy(
            src_ref=owned.at[spot(g, peer)],
            dst_ref=back.at[block(column)],
            send_sem=returned.at[columns + k],
            recv_sem=returned.at[k],
            device_id=(me, peer),
            device_id_type=MESH,
        )

    quarter = share // 2
    tile = 512

    def parts(g):
        base = g * share
        return pl.ds(base, quarter), pl.ds(base + quarter, quarter), pl.ds(base, share)

    class Gather:
        def __init__(self, g):
            self.low, self.high, self.all = parts(g)
            low, high = self.low, self.high
            self.up_low = copies.start(x.at[0, 0, low], x.at[3, 0, low], (up, column))
            self.down_high = copies.start(x.at[0, 0, high], x.at[1, 0, high], (down, column))
            self.up_high = copies.start(x.at[0, 0, high], x.at[3, 0, high], (up, column))
            self.down_low = copies.start(x.at[0, 0, low], x.at[1, 0, low], (down, column))
            self.share0 = copies.start(x.at[0, 0, self.all], x.at[0, 1, self.all], (pair, column))

        def forward(self):
            low, high = self.low, self.high
            self.up_low.wait_recv()
            self.pass_up = copies.start(x.at[3, 0, low], x.at[2, 0, low], (up, column))
            self.down_high.wait_recv()
            self.pass_down = copies.start(x.at[1, 0, high], x.at[2, 0, high], (down, column))

        def near(self):
            rows = self.all
            self.up_high.wait_recv()
            self.share3 = copies.start(x.at[3, 0, rows], x.at[3, 1, rows], (pair, column))
            self.down_low.wait_recv()
            self.share1 = copies.start(x.at[1, 0, rows], x.at[1, 1, rows], (pair, column))

        def far(self):
            low, high = self.low, self.high
            self.pass_up.wait_recv()
            self.share_low = copies.start(x.at[2, 0, low], x.at[2, 1, low], (pair, column))
            self.pass_down.wait_recv()
            self.share_high = copies.start(x.at[2, 0, high], x.at[2, 1, high], (pair, column))

    def grow(g, ks):
        rows = parts(g)[2]
        sums[...] = jnp.zeros_like(sums)

        def step(i, carry):
            lanes = pl.ds(pl.multiple_of(i * tile, tile), tile)
            left = jnp.concatenate([x[k, r, rows, lanes] for k in ks for r in (0, 1)], 0)
            sums[...] += dot(left, up_w[lanes, :])
            return carry

        lax.fori_loop(0, width // tile, step, 0)
        total = sums[...]
        hidden[...] = (total / (1.0 + jnp.exp(-total))).astype(BF16)

    def shrink(g, ks):
        rows = parts(g)[2]

        def step(i, carry):
            lanes = pl.ds(pl.multiple_of(i * tile, tile), tile)
            part = dot(hidden[...], down_w[:, lanes]).astype(BF16)
            for n, k in enumerate(ks):
                mine[k, rows, lanes] = part[2 * n * share : (2 * n + 1) * share]
                theirs[k, rows, lanes] = part[(2 * n + 1) * share : (2 * n + 2) * share]
            return carry

        lax.fori_loop(0, width // tile, step, 0)

    def add(target, spot, *terms):
        def piece(i, carry):
            lanes = pl.ds(pl.multiple_of(i * tile, tile), tile)
            total = terms[0][0][terms[0][1] + (lanes,)].astype(F32)
            for ref, at in terms[1:]:
                total += ref[at + (lanes,)].astype(F32)
            target[spot + (lanes,)] = total.astype(BF16)
            return carry

        lax.fori_loop(0, width // tile, piece, 0)

    class Reduce:
        def __init__(self, g):
            self.g = g
            self.low, self.high, self.all = parts(g)
            self.given = {}

        def give(self, k):
            self.given[k] = copies.start(theirs.at[k, self.all], others.at[k, self.all], (pair, column))

        def join(self, k, rows, *more):
            add(mine, (k, rows), (mine, (k, rows)), (others, (k, rows)), *more)

        def begin(self):
            low, high, g = self.low, self.high, self.g
            self.given[2].wait_recv()
            self.join(2, low)
            self.relay_up = copies.start(mine.at[2, low], relay.at[g, 0], (up, column))
            self.join(2, high)
            self.relay_down = copies.start(mine.at[2, high], relay.at[g, 1], (down, column))
            self.given[1].wait_recv()
            self.join(1, high)
            self.sent1 = copies.start(mine.at[1, high], ring.at[0, high], (up, column))
            self.given[3].wait_recv()
            self.join(3, low)
            self.sent3 = copies.start(mine.at[3, low], ring.at[1, low], (down, column))

        def relayed(self):
            low, high, g = self.low, self.high, self.g
            every = pl.ds(0, quarter)
            self.relay_up.wait_recv()
            self.join(1, low, (relay, (g, 0, every)))
            self.last1 = copies.start(mine.at[1, low], ring.at[0, low], (up, column))
            self.relay_down.wait_recv()
            self.join(3, high, (relay, (g, 1, every)))
            self.last3 = copies.start(mine.at[3, high], ring.at[1, high], (down, column))
            self.given[0].wait_recv()
            self.join(0, self.all)

        def end(self):
            rows = self.all
            for copy in (self.sent1, self.sent3, self.last1, self.last3):
                copy.wait_recv()
            add(owned, (rows,), (mine, (0, rows)), (ring, (0, rows)), (ring, (1, rows)))
            for k in members[self.g]:
                if k == 0:
                    source = owned.at[spot(self.g, column)]
                    pltpu.make_async_copy(source, back.at[block(column)], returned.at[0]).start()
                else:
                    sending(self.g, k).start()

    deal(0)
    chosen = [jnp.sum(logits * h, axis=0, keepdims=True) for h in hot]
    opened = [1.0 / (1.0 + jnp.exp(-v)) for v in chosen]
    both = opened[0] + opened[1]
    gates = split(picks[0] * (opened[0] / both) + picks[1] * (opened[1] / both))
    dealt_all(0)
    gather0 = Gather(0)
    deal(1)
    for load in loads[-2:]:
        load.wait()
    gather0.forward()
    dealt_all(1)
    gather1 = Gather(1)
    gather0.near()
    gather0.share0.wait_recv()
    gather0.share3.wait_recv()
    grow(0, (0, 3))
    shrink(0, (0, 3))
    reduce0 = Reduce(0)
    reduce0.give(0)
    reduce0.give(3)
    gather0.far()
    gather0.share1.wait_recv()
    gather0.share_low.wait_recv()
    gather0.share_high.wait_recv()
    grow(0, (2, 1))
    gather1.forward()
    gather1.near()
    shrink(0, (2, 1))
    reduce0.give(2)
    reduce0.give(1)
    reduce0.begin()
    gather1.share0.wait_recv()
    gather1.share3.wait_recv()
    grow(1, (0, 3))
    gather1.far()
    shrink(1, (0, 3))
    reduce1 = Reduce(1)
    reduce1.give(0)
    reduce1.give(3)
    reduce0.relayed()
    gather1.share1.wait_recv()
    gather1.share_low.wait_recv()
    gather1.share_high.wait_recv()
    grow(1, (2, 1))
    shrink(1, (2, 1))
    reduce1.give(2)
    reduce1.give(1)
    reduce1.begin()
    reduce0.end()
    reduce1.relayed()
    reduce1.end()

    for k in range(columns):
        rows = back.at[block(from_offset(k))]
        pltpu.make_async_copy(rows, rows, returned.at[k]).wait()

    def combine(i, carry):
        lanes = pl.ds(pl.multiple_of(i * tile, tile), tile)
        rows = back[:, lanes]
        total = dot(gates[0], rows, ((0,), (0,))) + dot(gates[1], rows, ((0,), (0,)))
        out_ref[:, lanes] = (mixed_ref[:, lanes].astype(F32) + total).astype(BF16)
        return carry

    lax.fori_loop(0, width // tile, combine, 0)
    copies.finish()
    for g in range(GROUPS):
        for k in members[g]:
            if k > 0:
                dealing(g, k).wait_send()
                sending(g, k).wait_send()


def leave_kernel(out_ref, final_ref, out_to, final_to, out_part, final_part, sems):
    pairs = []
    for source, through, target in ((out_ref, out_part, out_to), (final_ref, final_part, final_to)):
        rows = source.shape[0] // 2
        for n in range(2):
            part = pl.ds(n * rows, rows)
            at = len(pairs)
            pairs.append(
                (
                    pltpu.make_async_copy(source.at[part], through.at[part], sems.at[at]),
                    pltpu.make_async_copy(through.at[part], target.at[part], sems.at[4 + at]),
                )
            )
    for arrive, _ in pairs:
        arrive.start()
    for arrive, leave in pairs:
        arrive.wait()
        leave.start()
    for _, leave in pairs:
        leave.wait()


COPIES = 22 + GROUPS * (5 + 2 + 2 + 2 + 4 + 6)


def local(
    tokens,
    queries,
    keys_values,
    scan_input,
    state_maps,
    step_size,
    step_decay,
    block_pool,
    state_pool,
    block_holder,
    block_index,
    cached_blocks,
    state_holder,
    state_index,
    norm_gain,
    router_weight,
    expert_ids,
    up_weight,
    down_weight,
):
    length, width = tokens.shape
    experts = router_weight.shape[1]
    chips = lax.axis_size("dp") // 2
    columns = lax.axis_size("expert")
    pool_rows, state_rows = block_pool.shape[0], state_pool.shape[0]
    entries = block_holder.shape[1]
    kv = keys_values.shape[1]
    states = state_pool.reshape(state_rows, -1, 128).transpose(1, 0, 2)
    flat = states.shape[0]
    vmem = pl.BlockSpec(memory_space=pltpu.VMEM)
    hbm = pl.BlockSpec(memory_space=pltpu.HBM)
    dma = pltpu.SemaphoreType.DMA
    hidden = up_weight.shape[2]
    count = experts * CAP

    def like(array):
        return pltpu.VMEM(array.shape, array.dtype)

    maps, gain, router, ids = state_maps.T, norm_gain[None, :], router_weight.T, expert_ids.T
    layer_out, final = pl.pallas_call(
        layer_kernel,
        out_shape=(
            jax.ShapeDtypeStruct((length, width), BF16),
            jax.ShapeDtypeStruct((flat, 128), F32),
        ),
        in_specs=[hbm] * 19,
        out_specs=(vmem, vmem),
        scratch_shapes=[
            pltpu.SMEM(block_holder.shape, jnp.int32),
            pltpu.SMEM(block_index.shape, jnp.int32),
            pltpu.SMEM(cached_blocks.shape, jnp.int32),
            pltpu.SMEM(state_holder.shape, jnp.int32),
            pltpu.SMEM(state_index.shape, jnp.int32),
            like(tokens),
            like(queries),
            like(scan_input),
            like(maps),
            like(step_size),
            like(step_decay),
            like(gain),
            like(router),
            like(ids),
            like(states),
            pltpu.VMEM((chips, 2, pool_rows, BLOCK, kv), BF16),
            pltpu.VMEM((chips, 2, state_rows, flat, 128), BF16),
            pltpu.VMEM((entries * BLOCK + length, kv), BF16),
            pltpu.VMEM((length, width), F32),
            pltpu.VMEM((length, width), BF16),
            pltpu.VMEM((count, width), BF16),
            pltpu.VMEM((width, hidden), BF16),
            pltpu.VMEM((hidden, width), BF16),
            pltpu.VMEM((chips, 2, count, width), BF16),
            pltpu.VMEM((4 * count // GROUPS, hidden), F32),
            pltpu.VMEM((4 * count // GROUPS, hidden), BF16),
            pltpu.VMEM((chips, count, width), BF16),
            pltpu.VMEM((chips, count, width), BF16),
            pltpu.VMEM((chips, count, width), BF16),
            pltpu.VMEM((GROUPS, 2, count // GROUPS // 2, width), BF16),
            pltpu.VMEM((2, count, width), BF16),
            pltpu.VMEM((count, width), BF16),
            pltpu.VMEM((count, width), BF16),
            dma((COPIES,)),
            dma((COPIES,)),
            dma((2 * columns,)),
            dma((2 * columns,)),
            dma((19,)),
        ],
        compiler_params=pltpu.CompilerParams(
            collective_id=0, has_side_effects=True, vmem_limit_bytes=60 << 20
        ),
        name="layer",
    )(
        block_holder,
        block_index,
        cached_blocks,
        state_holder,
        state_index,
        tokens,
        queries,
        keys_values,
        scan_input,
        maps,
        step_size,
        step_decay,
        block_pool,
        states,
        gain,
        router,
        ids,
        up_weight,
        down_weight,
    )
    layer_out, final = pl.pallas_call(
        leave_kernel,
        out_shape=(
            jax.ShapeDtypeStruct(layer_out.shape, BF16),
            jax.ShapeDtypeStruct(final.shape, F32),
        ),
        in_specs=[hbm, hbm],
        out_specs=(hbm, hbm),
        scratch_shapes=[like(layer_out), like(final), dma((8,))],
        name="leave",
    )(layer_out, final)
    return (layer_out, final.reshape(1, -1))


def solution(mesh):
    placed = (
        P(("dp", "expert"), None),
        P(("dp", "expert"), None),
        P(("dp", "expert"), None),
        P(("dp", "expert"), None),
        P(("dp", "expert"), None),
        P(("dp", "expert"), None),
        P(("dp", "expert"), None),
        P(("dp", "expert"), None, None),
        P(("dp", "expert"), None),
        P(("dp", "expert"), None),
        P(("dp", "expert"), None),
        P(("dp", "expert")),
        P(("dp", "expert")),
        P(("dp", "expert")),
        P(),
        P(),
        P(("dp", "expert"), None),
        P("expert", None, "dp"),
        P("expert", "dp", None),
    )
    return jax.shard_map(
        local,
        mesh=mesh,
        in_specs=placed,
        out_specs=(P(("dp", "expert"), None), P(("dp", "expert"), None)),
        check_vma=False,
    )
```

time: 273 us -> 143 us (0.52)
  Pallas kernels: 0 us -> 141 us
  waiting for transfers between devices: 118 us -> 0 us
  local copies, waits for them, and re-layouts: 40.1 us -> 0 us
  matrix products: 39.5 us -> 0 us
  blocking collectives: 23.7 us -> 0 us
  starting transfers between devices: 17.5 us -> 0 us
  other arithmetic: 17.4 us -> 0 us
  between operations: 16.2 us -> 2.58 us
    pallas_call x0 -> x2, Pallas kernels: none -> 141 us  [the longest x1 139 us: local(): pl.pallas_call(layer_kernel, out_shape=(jax.ShapeDtypeStruct((length, wid...]
    reduce_scatter x1 -> x0, waiting for transfers between devices: 51.6 us -> none  [local(): lax.psum_scatter(apply_expert(gathered, up_local, down_local).astype(jnp....]
    all_gather x2 -> x0, waiting for transfers between devices: 46.6 us -> none  [the longest x1 46.6 us: local(): gathered = lax.all_gather(received, 'dp', axis=0, tiled=True)]
    dot_general x9 -> x0, matrix products: 39.5 us -> none  [the longest x1 14.1 us: apply_expert(): jnp.dot(hidden, down_local, preferred_element_type=jnp.float32)]
    all_to_all x1 -> x0, blocking collectives: 23.7 us -> none  [local(): lax.all_to_all(dispatch, 'expert', split_axis=0, concat_axis=0, tiled=True)]
    all_to_all x3 -> x0, waiting for transfers between devices: 18.9 us -> none  [the longest x1 14.1 us: local(): lax.all_to_all(sent_states.astype(jnp.bfloat16), 'dp', split_axis=0, conc...]
    all_to_all x3 -> x0, starting transfers between devices: 17.2 us -> none  [the longest x1 6.87 us: local(): lax.all_to_all(own_sums.astype(jnp.bfloat16), 'expert', split_axis=0, con...]
    gather x9 -> x0, local copies, waits for them, and re-layouts: 9.81 us -> none  [the longest x1 2.92 us: local(): prefix = pooled[row_ids]]
  transfers between devices with their start and end apart: 6 -> 0, of which waited for: 4 -> 0; matrix products, arithmetic and copies ran while one was open for 16% -> 0% of each run, Pallas kernels for 0% -> 0%
where the time goes in v2:
time: 143 us
  Pallas kernels  141 us (99%)
  between operations  2.58 us (2%)
    pallas_call x1, Pallas kernels, local(): pl.pallas_call(layer_kernel, out_shape=(jax.ShapeDtypeStruct((length, wid...  139 us

profile of v2, /device:TPU:0, one launch (start us, length us, event | category | flops | bytes accessed | tf_op | source)
XLA Modules:
  0.0 143.2 jit_solution(10986456368192053849)
XLA Ops:
  2.6 138.7 %layer.1 = (bf16[64,4096]{1,0:T(8,128)(2,1)}, f32[512,128]{1,0:T(8,128)}) custom-call(s32[1,16]{1,0:T(1,128)} %holder_hbm.1, s32[1,16]{1,0:T(1,128)} %index_hbm.1, s32[1]{0:T(128)S(6)} %copy.21.count_hbm, s32[1]{0:T(128)S(6)} %copy.22.owner_hbm, s32[1]{0:T(128)S(6)} %copy.23.state_row_hbm, bf16[64,4096]{1,0:T(8,128)(2,1)} %tokens_hbm.1, ...), custom_call_target="tpu_custom_call" | custom-call | tf_op jit(solution)/shard_map/layer/pallas_call | solution.py:644
  141.3 1.9 %leave.1 = (bf16[64,4096]{1,0:T(8,128)(2,1)}, f32[512,128]{1,0:T(8,128)}) custom-call(bf16[64,4096]{1,0:T(8,128)(2,1)} %get-tuple-element.6.out_ref, f32[512,128]{1,0:T(8,128)} %get-tuple-element.7.final_ref), custom_call_target="tpu_custom_call" | custom-call | tf_op jit(solution)/shard_map/leave/pallas_call | solution.py:717

commit v3 on v2

--- a/solution.py
+++ b/solution.py
@@ -63,7 +63,7 @@
             copy.wait_send()
 
 
-GROUPS = 2
+GROUPS = 4
 
 
 def layer_kernel(
@@ -325,7 +325,7 @@
     share = columns // GROUPS * CAP
     row, place_in_row = column // side_len, lax.rem(column, side_len)
     offsets = [(k // side_len, k % side_len) for k in range(columns)]
-    members = [[k for k, (a, b) in enumerate(offsets) if (a + b) % GROUPS == g] for g in range(GROUPS)]
+    members = [[k for k, (a, b) in enumerate(offsets) if a % 2 * 2 + b % 2 == g] for g in range(GROUPS)]
 
     def at_offset(k):
         along, across = offsets[k]
@@ -337,7 +337,8 @@
         return there * side_len + lax.rem(place_in_row + side_len - across, side_len)
 
     def spot(g, source):
-        return pl.ds(pl.multiple_of(g * share + source // GROUPS * CAP, CAP), CAP)
+        at = source // (2 * side_len) * (side_len // 2) + lax.rem(source, side_len) // 2
+        return pl.ds(pl.multiple_of(g * share + at * CAP, CAP), CAP)
 
     def block(other):
         return pl.ds(pl.multiple_of(other * CAP, CAP), CAP)
@@ -378,7 +379,7 @@
         )
 
     quarter = share // 2
-    tile = 512
+    tile, wide_tile = 1024, 2048
 
     def parts(g):
         base = g * share
@@ -444,14 +445,14 @@
 
     def add(target, spot, *terms):
         def piece(i, carry):
-            lanes = pl.ds(pl.multiple_of(i * tile, tile), tile)
+            lanes = pl.ds(pl.multiple_of(i * wide_tile, wide_tile), wide_tile)
             total = terms[0][0][terms[0][1] + (lanes,)].astype(F32)
             for ref, at in terms[1:]:
                 total += ref[at + (lanes,)].astype(F32)
             target[spot + (lanes,)] = total.astype(BF16)
             return carry
 
-        lax.fori_loop(0, width // tile, piece, 0)
+        lax.fori_loop(0, width // wide_tile, piece, 0)
 
     class Reduce:
         def __init__(self, g):
@@ -508,53 +509,65 @@
     opened = [1.0 / (1.0 + jnp.exp(-v)) for v in chosen]
     both = opened[0] + opened[1]
     gates = split(picks[0] * (opened[0] / both) + picks[1] * (opened[1] / both))
-    dealt_all(0)
-    gather0 = Gather(0)
-    deal(1)
+    gathers, reduces = [], [Reduce(g) for g in range(GROUPS)]
+
+    def open_gather(g):
+        dealt_all(g)
+        gathers.append(Gather(g))
+        if g + 1 < GROUPS:
+            deal(g + 1)
+
+    every = (0, 1, 2, 3)
+
+    def up_half(g):
+        gather = gathers[g]
+        for copy in (gather.share0, gather.share1, gather.share3, gather.share_low, gather.share_high):
+            copy.wait_recv()
+        grow(g, every)
+
+    def down_half(g):
+        shrink(g, every)
+        for k in (2, 1, 3, 0):
+            reduces[g].give(k)
+
+    open_gather(0)
+    gathers[0].forward()
+    open_gather(1)
+    gathers[0].near()
+    gathers[1].forward()
+    open_gather(2)
+    gathers[0].far()
+    gathers[1].near()
+    gathers[2].forward()
     for load in loads[-2:]:
         load.wait()
-    gather0.forward()
-    dealt_all(1)
-    gather1 = Gather(1)
-    gather0.near()
-    gather0.share0.wait_recv()
-    gather0.share3.wait_recv()
-    grow(0, (0, 3))
-    shrink(0, (0, 3))
-    reduce0 = Reduce(0)
-    reduce0.give(0)
-    reduce0.give(3)
-    gather0.far()
-    gather0.share1.wait_recv()
-    gather0.share_low.wait_recv()
-    gather0.share_high.wait_recv()
-    grow(0, (2, 1))
-    gather1.forward()
-    gather1.near()
-    shrink(0, (2, 1))
-    reduce0.give(2)
-    reduce0.give(1)
-    reduce0.begin()
-    gather1.share0.wait_recv()
-    gather1.share3.wait_recv()
-    grow(1, (0, 3))
-    gather1.far()
-    shrink(1, (0, 3))
-    reduce1 = Reduce(1)
-    reduce1.give(0)
-    reduce1.give(3)
-    reduce0.relayed()
-    gather1.share1.wait_recv()
-    gather1.share_low.wait_recv()
-    gather1.share_high.wait_recv()
-    grow(1, (2, 1))
-    shrink(1, (2, 1))
-    reduce1.give(2)
-    reduce1.give(1)
-    reduce1.begin()
-    reduce0.end()
-    reduce1.relayed()
-    reduce1.end()
+    open_gather(3)
+    up_half(0)
+    gathers[3].forward()
+    gathers[1].far()
+    gathers[2].near()
+    down_half(0)
+    reduces[0].begin()
+    up_half(1)
+    gathers[2].far()
+    gathers[3].near()
+    down_half(1)
+    reduces[1].begin()
+    reduces[0].relayed()
+    up_half(2)
+    gathers[3].far()
+    down_half(2)
+    reduces[2].begin()
+    reduces[1].relayed()
+    up_half(3)
+    down_half(3)
+    reduces[3].begin()
+    reduces[0].end()
+    reduces[2].relayed()
+    reduces[1].end()
+    reduces[3].relayed()
+    reduces[2].end()
+    reduces[3].end()
 
     for k in range(columns):
         rows = back.at[block(from_offset(k))]
@@ -674,8 +687,8 @@
             pltpu.VMEM((width, hidden), BF16),
             pltpu.VMEM((hidden, width), BF16),
             pltpu.VMEM((chips, 2, count, width), BF16),
-            pltpu.VMEM((4 * count // GROUPS, hidden), F32),
-            pltpu.VMEM((4 * count // GROUPS, hidden), BF16),
+            pltpu.VMEM((2 * chips * count // GROUPS, hidden), F32),
+            pltpu.VMEM((2 * chips * count // GROUPS, hidden), BF16),
             pltpu.VMEM((chips, count, width), BF16),
             pltpu.VMEM((chips, count, width), BF16),
             pltpu.VMEM((chips, count, width), BF16),

time: 143 us -> 139 us (0.972)
  Pallas kernels: 141 us -> 136 us
    pallas_call x1, Pallas kernels: 139 us -> 134 us  [local(): pl.pallas_call(layer_kernel, out_shape=(jax.ShapeDtypeStruct((length, wid...]
where the time goes in v3:
time: 139 us
  Pallas kernels  136 us (98%)
  between operations  2.58 us (2%)
    pallas_call x1, Pallas kernels, local(): pl.pallas_call(layer_kernel, out_shape=(jax.ShapeDtypeStruct((length, wid...  134 us

profile of v3, /device:TPU:0, one launch (start us, length us, event | category | flops | bytes accessed | tf_op | source)
XLA Modules:
  0.0 138.8 jit_solution(13179351748193375248)
XLA Ops:
  2.6 134.4 %layer.1 = (bf16[64,4096]{1,0:T(8,128)(2,1)}, f32[512,128]{1,0:T(8,128)}) custom-call(s32[1,16]{1,0:T(1,128)} %holder_hbm.1, s32[1,16]{1,0:T(1,128)} %index_hbm.1, s32[1]{0:T(128)S(6)} %copy.21.count_hbm, s32[1]{0:T(128)S(6)} %copy.22.owner_hbm, s32[1]{0:T(128)S(6)} %copy.23.state_row_hbm, bf16[64,4096]{1,0:T(8,128)(2,1)} %tokens_hbm.1, ...), custom_call_target="tpu_custom_call" | custom-call | tf_op jit(solution)/shard_map/layer/pallas_call | solution.py:657
  136.9 1.9 %leave.1 = (bf16[64,4096]{1,0:T(8,128)(2,1)}, f32[512,128]{1,0:T(8,128)}) custom-call(bf16[64,4096]{1,0:T(8,128)(2,1)} %get-tuple-element.6.out_ref, f32[512,128]{1,0:T(8,128)} %get-tuple-element.7.final_ref), custom_call_target="tpu_custom_call" | custom-call | tf_op jit(solution)/shard_map/leave/pallas_call | solution.py:730

commit v4 on v3

--- a/solution.py
+++ b/solution.py
@@ -174,24 +174,42 @@
 
     copies = Copies(send, recv)
     half = pools.shape[2] // 2
-    first, second = pl.ds(0, half), pl.ds(half, half)
-    kinds = (
-        (pools.at[0, 0], pools, first, second),
-        (starts.at[0, 0], starts, pl.ds(0, 1), pl.ds(1, 1)),
-    )
+
+    class Spread:
+        def __init__(self, store, low, high):
+            self.store, self.low, self.high = store, low, high
+            self.up_low = copies.start(store.at[0, 0, low], store.at[3, 0, low], (up, column))
+            self.down_high = copies.start(store.at[0, 0, high], store.at[1, 0, high], (down, column))
+            self.up_high = copies.start(store.at[0, 0, high], store.at[3, 0, high], (up, column))
+            self.down_low = copies.start(store.at[0, 0, low], store.at[1, 0, low], (down, column))
+            self.shared = [copies.start(store.at[0, 0], store.at[0, 1], (pair, column))]
+
+        def share(self, *at):
+            self.shared.append(
+                copies.start(self.store.at[(at[0], 0) + at[1:]], self.store.at[(at[0], 1) + at[1:]], (pair, column))
+            )
+
+        def forward(self):
+            store, low, high = self.store, self.low, self.high
+            self.up_low.wait_recv()
+            self.pass_up = copies.start(store.at[3, 0, low], store.at[2, 0, low], (up, column))
+            self.down_high.wait_recv()
+            self.pass_down = copies.start(store.at[1, 0, high], store.at[2, 0, high], (down, column))
+
+        def finish(self):
+            self.up_high.wait_recv()
+            self.share(3)
+            self.down_low.wait_recv()
+            self.share(1)
+            self.pass_up.wait_recv()
+            self.share(2, self.low)
+            self.pass_down.wait_recv()
+            self.share(2, self.high)
+            for copy in self.shared:
+                copy.wait_recv()
+
     loads[0].wait()
-    loads[1].wait()
-    for n in range(states_ref.shape[1]):
-        starts[0, 0, n] = states_ref[:, n, :].astype(BF16)
-    to_up, to_down, shared = [], [], []
-    for own, store, low, high in kinds:
-        to_up.append(copies.start(own.at[low], store.at[3, 0, low], (up, column)))
-        to_down.append(copies.start(own.at[high], store.at[1, 0, high], (down, column)))
-    for own, store, low, high in kinds:
-        to_up.append(copies.start(own.at[high], store.at[3, 0, high], (up, column)))
-        to_down.append(copies.start(own.at[low], store.at[1, 0, low], (down, column)))
-    for own, store, low, high in kinds:
-        shared.append(copies.start(own, store.at[0, 1], (pair, column)))
+    blocks = Spread(pools, pl.ds(0, half), pl.ds(half, half))
 
     for load in loads[2:7]:
         load.wait()
@@ -240,26 +258,14 @@
 
     lax.fori_loop(0, width // span, scan, 0)
 
-    passed = []
-    for n, (own, store, low, high) in enumerate(kinds):
-        to_up[n].wait_recv()
-        passed.append(copies.start(store.at[3, 0, low], store.at[2, 0, low], (up, column)))
-        to_down[n].wait_recv()
-        passed.append(copies.start(store.at[1, 0, high], store.at[2, 0, high], (down, column)))
-    for n, (own, store, low, high) in enumerate(kinds):
-        to_up[2 + n].wait_recv()
-        shared.append(copies.start(store.at[3, 0], store.at[3, 1], (pair, column)))
-        to_down[2 + n].wait_recv()
-        shared.append(copies.start(store.at[1, 0], store.at[1, 1], (pair, column)))
-    for n, (own, store, low, high) in enumerate(kinds):
-        passed[2 * n].wait_recv()
-        shared.append(copies.start(store.at[2, 0, low], store.at[2, 1, low], (pair, column)))
-        passed[2 * n + 1].wait_recv()
-        shared.append(copies.start(store.at[2, 0, high], store.at[2, 1, high], (pair, column)))
+    loads[1].wait()
+    for n in range(states_ref.shape[1]):
+        starts[0, 0, n] = states_ref[:, n, :].astype(BF16)
+    blocks.forward()
+    states = Spread(starts, pl.ds(0, 1), pl.ds(1, 1))
     for load in loads[7:-2]:
         load.wait()
-    for copy in shared:
-        copy.wait_recv()
+    blocks.finish()
     for load in loads[-2:]:
         load.start()
 
@@ -280,7 +286,7 @@
     kv_width = KV_HEADS * HEAD
     ending = decayed[length - 1 : length]
 
-    def chunk(g, total):
+    def attend(g):
         lanes = pl.ds(g * span, span)
         query = queries_ref[:, lanes]
         query = jnp.concatenate([query[:, j * HEAD : (j + 1) * HEAD] for j in range(groups)], 0)
@@ -291,23 +297,31 @@
         weights = (weights / jnp.sum(weights, axis=1, keepdims=True)).astype(BF16)
         attended = dot(weights, value)
         attended = jnp.concatenate([attended[j * length : (j + 1) * length] for j in range(groups)], 1)
-
+        wide[:, lanes] += attended
+
+    def settle(g, total):
+        lanes = pl.ds(g * span, span)
         part = pl.ds(g * depth, depth)
         start = starts[side, other, state_row, part, :]
         channels = (dot(unpack, start) * lane_kept).astype(BF16)
         started = dot(readout_rows, channels, ((1,), (1,)))
-        scanned = wide[:, lanes] + dot(fade, spread_of(g)) * started
+        mixers = wide[:, lanes] + dot(fade, spread_of(g)) * started
         owner = g * (span // SSM_DIM) + iota((depth, heads), 0) // (SSM_DIM // packed)
         ended = jnp.sum(jnp.where(iota((depth, heads), 1) == owner, ending, 0.0), axis=1, keepdims=True)
         final_ref[part, :] = ended * (start.astype(F32) + final_ref[part, :])
-        mixed = (tokens_ref[:, lanes].astype(F32) + (attended + scanned)).astype(BF16)
+        mixed = (tokens_ref[:, lanes].astype(F32) + mixers).astype(BF16)
         mixed_ref[:, lanes] = mixed
         mixed = mixed.astype(F32)
         return total + jnp.sum(mixed * mixed, axis=1, keepdims=True)
 
     total = jnp.zeros((length, 1), F32)
     for g in range(width // span):
-        total = chunk(g, total)
+        if g == width // span // 2:
+            states.forward()
+        attend(g)
+    states.finish()
+    for g in range(width // span):
+        total = settle(g, total)
     scale = lax.rsqrt(total / width + 1e-05)
     pick = (picks[0] + picks[1]).astype(BF16)
 

time: 139 us -> 135 us (0.971)
  Pallas kernels: 136 us -> 132 us
    pallas_call x1, Pallas kernels: 134 us -> 131 us  [local(): pl.pallas_call(layer_kernel, out_shape=(jax.ShapeDtypeStruct((length, wid...]
where the time goes in v4:
time: 135 us
  Pallas kernels  132 us (98%)
  between operations  2.58 us (2%)
    pallas_call x1, Pallas kernels, local(): pl.pallas_call(layer_kernel, out_shape=(jax.ShapeDtypeStruct((length, wid...  131 us

profile of v4, /device:TPU:0, one launch (start us, length us, event | category | flops | bytes accessed | tf_op | source)
XLA Modules:
  0.0 135.1 jit_solution(15777515677103720847)
XLA Ops:
  2.6 130.6 %layer.1 = (bf16[64,4096]{1,0:T(8,128)(2,1)}, f32[512,128]{1,0:T(8,128)}) custom-call(s32[1,16]{1,0:T(1,128)} %holder_hbm.1, s32[1,16]{1,0:T(1,128)} %index_hbm.1, s32[1]{0:T(128)S(6)} %copy.21.count_hbm, s32[1]{0:T(128)S(6)} %copy.22.owner_hbm, s32[1]{0:T(128)S(6)} %copy.23.state_row_hbm, bf16[64,4096]{1,0:T(8,128)(2,1)} %tokens_hbm.1, ...), custom_call_target="tpu_custom_call" | custom-call | tf_op jit(solution)/shard_map/layer/pallas_call | solution.py:671
  133.2 1.9 %leave.1 = (bf16[64,4096]{1,0:T(8,128)(2,1)}, f32[512,128]{1,0:T(8,128)}) custom-call(bf16[64,4096]{1,0:T(8,128)(2,1)} %get-tuple-element.6.out_ref, f32[512,128]{1,0:T(8,128)} %get-tuple-element.7.final_ref), custom_call_target="tpu_custom_call" | custom-call | tf_op jit(solution)/shard_map/leave/pallas_call | solution.py:744
